TPU v7x, 128 devices: a whole 4x4x4 slice. The times are simulated.
128 devices in a mesh: dp: 2 (over x_lo), phase: 16 (over z, y), tensor: 4 (over x_hi, core).
Axes of the slice: x: 4 (x_hi: 2, x_lo: 2; x = x_hi * 2 + x_lo), y: 4, z: 4, core: 2. Of those that a mesh axis runs over, the one named last changes fastest.
Arguments:
- tokens: bfloat16 [2, 2048, 8192], P('dp', 'phase', 'tensor'), may hold values from -6 to 6
- bc_proj: bfloat16 [2, 2048, 2, 2048], P('dp', 'phase', None, 'tensor'), may hold values from -0.3984375 to 0.3984375
- step_sizes: bfloat16 [2, 256, 1024], P('dp', 'phase', 'tensor'), may hold values from 0.5 to 2
- decay_rates: float32 [128], P('tensor'), may hold values from 6.1035156e-05 to 0.02
- direct_weight: float32 [128], P('tensor'), may hold values from 0.5 to 1.5
- norm_gain: float32 [8192], P('tensor'), may hold values from 0.1 to 1.9
- routes: int32 [2, 256, 1], P('dp', 'phase'), may hold values from 0 to 1; in each aligned block of 16 rows (0 to 15, 16 to 31, ..., all dimensions but the last counted through in order) at most 16 rows name the same one
- segments: int32 [2, 4096], P('dp', 'phase'), may hold values from 0 to 3, never falling along the last dimension, each value on 1 to 2048 neighbouring positions
Outputs:
- mixed: bfloat16 [2, 2048, 8192], P('dp', 'phase', 'tensor')
Inputs may be any that keep to these rules, and one draw needn't show every extreme that they name: `routes`: no device sends more than 16 of its blocks to one data group. `segments`: document ids never fall along a row; each document covers 1 to 2048 positions, and one covers exactly 2048.
All inputs are finite; a program needn't handle non-finite values.
Results may differ from a plain program's by a relative error of at most 0.0075.
Values may be sent and summed in bfloat16 or wider, within the bound.
No kernel may reach another device: no remote copies, remote signals or barrier semaphores. Data moves between devices by JAX's collectives and lax.ppermute only.
A program may use at most 128 MiB of HBM per device.

v0:
```python
import jax
import jax.numpy as jnp
from jax import lax
from jax.experimental import pallas as pl
from jax.experimental.pallas import tpu as pltpu
from jax.sharding import Mesh, PartitionSpec as P


EPSILON = 1e-05
F32 = jnp.float32
BF16 = jnp.bfloat16
HIGH = lax.Precision.HIGHEST
TOK = 128
PEERS = 8
SPAN = TOK * PEERS
WIDE = 256
AUX = 8


def dot(a, b, dims, precision=None):
    return lax.dot_general(a, b, (dims, ((), ())), precision=precision, preferred_element_type=F32)


def iota(shape, dim):
    return lax.broadcasted_iota(jnp.int32, shape, dim)


def ones_where(cond, dtype=F32):
    return jnp.where(cond, 1.0, 0.0).astype(dtype)


def pack_kernel(
    tok_ref, bc_ref, dt_ref, route_ref, seg_ref, out_ref, c_ref, bc_buf, dt_buf, route_buf, seg_buf, sems
):
    small = ((route_ref, route_buf), (dt_ref, dt_buf), (seg_ref, seg_buf), (bc_ref, bc_buf))
    copies = [pltpu.make_async_copy(a, b, sems.at[n]) for n, (a, b) in enumerate(small)]
    for o in range(PEERS):
        src = tok_ref.at[:, o * WIDE : (o + 1) * WIDE]
        copies.append(pltpu.make_async_copy(src, out_ref.at[o, 0:TOK, 0:WIDE], sems.at[4 + o]))
    for copy in copies:
        copy.start()
    for copy in copies[:3]:
        copy.wait()
    block_of = ones_where(iota((16, TOK), 1) // 8 == iota((16, TOK), 0), BF16)
    spread = dot(dt_buf[...], block_of, ((0,), (0,)))
    same_u = iota((256, TOK), 0) % 8 == iota((256, TOK), 1) % 8
    spread = jnp.where(same_u, spread, 0.0).astype(BF16)
    head_of = ones_where(iota((32, 256), 1) // 8 == iota((32, 256), 0), BF16)
    dt_rows = dot(head_of, spread, ((1,), (0,)))
    route = jnp.broadcast_to(route_buf[...].astype(F32), (TOK, 16)).astype(BF16)
    route_row = dot(route, block_of, ((1,), (0,)))
    route_col = dot(block_of, route, ((0,), (1,)))
    ahead = (route_row == route_col) & (iota((TOK, TOK), 0) < iota((TOK, TOK), 1))
    place = jnp.sum(ones_where(ahead), axis=0, keepdims=True) + (lax.axis_index("dp") * TOK).astype(F32)
    segs = seg_buf[...]
    lane = iota((1, TOK), 1)
    starts = jnp.zeros((1, TOK), F32)
    for k in range(3):
        starts = jnp.where(lane == k, jnp.sum(ones_where(segs < k + 1), axis=1, keepdims=True), starts)
    row = iota((AUX, TOK), 0)
    for o in range(PEERS):
        aux = jnp.where(row == 4, route_row[0:1], jnp.where(row == 5, place, starts))
        for h in range(4):
            aux = jnp.where(row == h, dt_rows[o * 4 + h : o * 4 + h + 1], aux)
        out_ref[o, TOK : TOK + AUX, :] = jnp.concatenate([aux.astype(BF16)] * 4, axis=1)
    copies[3].wait()
    for g in range(2):
        b = bc_buf[:, 0, g * WIDE : (g + 1) * WIDE]
        c = bc_buf[:, 1, g * WIDE : (g + 1) * WIDE]
        for o in range(g * 4, g * 4 + 4):
            out_ref[o, :TOK, WIDE : 2 * WIDE] = b
            c_ref[o] = c
    for copy in copies[4:]:
        copy.wait()


def rate_lanes(ref):
    lane = iota((1, WIDE), 1) // 64
    first = (lax.axis_index("dp") * 4 + lax.axis_index("y")) * 4
    out = jnp.full((1, WIDE), ref[first], F32)
    for h in range(1, 4):
        out = jnp.where(lane == h, ref[first + h], out)
    return out


def keys_of(r_ref):
    pick_route = ones_where(iota((AUX, TOK), 0) == 4, BF16)
    pick_place = ones_where(iota((AUX, TOK), 0) == 5, BF16)
    starts = [[None] * 3, [None] * 3]
    rows, cols = [], []
    for q in range(PEERS):
        y, j = q // 2, q % 2
        aux = r_ref[j * 4 + y, TOK : TOK + AUX, 0:TOK]
        auxf = aux.astype(F32)
        rows.append((auxf[4:5], auxf[5:6] + y * 256.0))
        cols.append((dot(aux, pick_route, ((0,), (0,))), dot(aux, pick_place, ((0,), (0,))) + y * 256.0))
        for k in range(3):
            n = auxf[6:7, k : k + 1]
            starts[j][k] = n if starts[j][k] is None else starts[j][k] + n

    def key_of(route, place):
        second = route > 0.5
        doc = 4.0 * route
        for k in range(3):
            doc = doc + ones_where(place >= jnp.where(second, starts[1][k], starts[0][k]))
        return doc

    first, last = [], []
    for d in range(2):
        first.append(sum(ones_where(starts[d][k] <= 0.0) for k in range(3)))
        last.append(sum(ones_where(starts[d][k] <= SPAN - 1.0) for k in range(3)))
    return [key_of(*p) for p in rows], [key_of(*p) for p in cols], first, last


def state_kernel(rate_ref, r_ref, e_ref, f_ref, xs_ref, m_ref, dt_ref, bm_ref):
    rate = rate_lanes(rate_ref)
    spread = ones_where(iota((AUX, WIDE), 1) // 64 == iota((AUX, WIDE), 0), BF16)
    key_rows, key_cols, _, last = keys_of(r_ref)
    causal = iota((TOK, TOK), 0) >= iota((TOK, TOK), 1)
    for i in range(PEERS):
        src = (i % 2) * 4 + i // 2
        dt_ref[i * TOK : (i + 1) * TOK, :] = dot(r_ref[src, TOK : TOK + AUX, 0:TOK], spread, ((0,), (0,))).astype(BF16)
        for jj in range(i + 1 + (i + 1) % 2):
            if jj > i:
                m = jnp.zeros((TOK, TOK), BF16)
            else:
                same = key_cols[i] == key_rows[jj]
                m = ones_where(same & causal if i == jj else same, BF16)
            m_ref[i * TOK : (i + 1) * TOK, jj * TOK : (jj + 1) * TOK] = m
        for d in range(2):
            lm = ones_where(key_cols[i] == last[d] + 4.0 * d, BF16)
            for half in range(2):
                bm_ref[d, i * TOK : (i + 1) * TOK, half * TOK : (half + 1) * TOK] = (
                    r_ref[src, :TOK, WIDE + half * TOK : WIDE + (half + 1) * TOK] * lm
                )
    for b in range(4):
        sl = slice(b * 256, (b + 1) * 256)
        total = dot(m_ref[sl, : (b + 1) * 256], dt_ref[: (b + 1) * 256, :], ((1,), (0,)))
        f_ref[sl, :] = jnp.exp(-rate * total)
        grow = jnp.exp(rate * total) * dt_ref[sl, :].astype(F32)
        for s in range(2):
            x = r_ref[s * 4 + b, :TOK, 0:WIDE].astype(F32)
            at = b * 256 + s * TOK
            xs_ref[at : at + TOK, :] = (x * grow[s * TOK : (s + 1) * TOK]).astype(BF16)
    row8 = iota((AUX, WIDE), 0)
    for d in range(2):
        total = jnp.zeros((AUX, WIDE), F32)
        for q in range(PEERS):
            lm = jnp.broadcast_to(ones_where(key_rows[q] == last[d] + 4.0 * d), (AUX, TOK)).astype(BF16)
            total = total + dot(lm, dt_ref[q * TOK : (q + 1) * TOK, :], ((1,), (0,)))
        through = jnp.exp(-rate * total)
        e = dot(bm_ref[d], xs_ref[...], ((0,), (0,))) * through[0:1]
        e_ref[d, 0:WIDE, :] = e.astype(BF16)
        e_ref[d, WIDE : WIDE + AUX, :] = jnp.where(row8 == 0, through, last[d]).astype(BF16)


def inside_kernel(weight_ref, r_ref, got_ref, f_ref, xs_ref, base_ref, cm_ref, meta_ref, b_ref, c_ref):
    weight = rate_lanes(weight_ref)
    key_rows, key_cols, first, _ = keys_of(r_ref)
    meta_ref[...] = jnp.where(iota((AUX, TOK), 0) == 0, first[0], first[1])
    for q in range(PEERS):
        src = (q % 2) * 4 + q // 2
        sl = slice(q * TOK, (q + 1) * TOK)
        b_ref[sl, :] = r_ref[src, :TOK, WIDE : 2 * WIDE]
        c = got_ref[src]
        c_ref[sl, :] = c
        for d in range(2):
            fm = ones_where(key_cols[q] == first[d] + 4.0 * d, BF16)
            for half in range(2):
                at = d * WIDE + half * TOK
                cm_ref[sl, at : at + TOK] = c[:, half * TOK : (half + 1) * TOK] * fm
    causal = iota((256, 256), 0) >= iota((256, 256), 1)
    for i in range(4):
        si = slice(i * 256, (i + 1) * 256)
        acc = jnp.zeros((256, WIDE), F32)
        keys = jnp.concatenate([jnp.concatenate([key_cols[2 * i + n]] * 2, axis=1) for n in range(2)], axis=0)
        for j in range(i + 1):
            sj = slice(j * 256, (j + 1) * 256)
            s = dot(c_ref[si, :], b_ref[sj, :], ((1,), (1,)))
            same = keys == jnp.concatenate(key_rows[2 * j : 2 * j + 2], axis=1)
            w = jnp.where(same & causal if i == j else same, s, 0.0).astype(BF16)
            acc = acc + dot(w, xs_ref[sj, :], ((1,), (0,)))
        acc = acc * f_ref[si, :]
        for s in range(2):
            x = r_ref[s * 4 + i, :TOK, 0:WIDE].astype(F32)
            at = i * 256 + s * TOK
            base_ref[at : at + TOK, :] = acc[s * TOK : (s + 1) * TOK] + weight * x


def carry_kernel(base_ref, f_ref, cm_ref, e1_ref, e2_ref, meta_ref, y_ref, h_ref):
    for d in range(2):
        first = meta_ref[d : d + 1, 0:1]
        joined1 = e1_ref[d, WIDE + 1 : WIDE + 2, :].astype(F32) == first
        joined2 = joined1 & (e2_ref[d, WIDE + 1 : WIDE + 2, :].astype(F32) == first)
        through = jnp.where(joined2, e1_ref[d, WIDE : WIDE + 1, :].astype(F32), 0.0)
        near = jnp.where(joined1, e1_ref[d, 0:WIDE, :].astype(F32), 0.0)
        h_ref[d * WIDE : (d + 1) * WIDE, :] = (near + through * e2_ref[d, 0:WIDE, :].astype(F32)).astype(BF16)
    for q in range(PEERS):
        sl = slice(q * TOK, (q + 1) * TOK)
        y = base_ref[sl, :] + f_ref[sl, :] * dot(cm_ref[sl, :], h_ref[...], ((1,), (0,)))
        y_ref[(q % 2) * 4 + q // 2] = y.astype(BF16)


def square_kernel(y_ref, s_ref):
    acc = jnp.zeros((TOK, WIDE), F32)
    for o in range(PEERS):
        v = y_ref[o].astype(F32)
        acc = acc + v * v
    s_ref[...] = dot(jnp.ones((AUX, WIDE), F32), acc, ((1,), (1,)), HIGH)


def scale_kernel(y_ref, s0_ref, s1_ref, s2_ref, s3_ref, gain_ref, out_ref, *, features):
    total = (s0_ref[...] + s1_ref[...]) + (s2_ref[...] + s3_ref[...])
    pick = ones_where(iota((AUX, TOK), 0) == 0)
    col = dot(total, pick, ((0,), (0,)), HIGH)
    scale = lax.rsqrt(col / features + EPSILON)
    scale = jnp.concatenate([scale, scale], axis=1)
    for o in range(PEERS):
        sl = slice(o * WIDE, (o + 1) * WIDE)
        out_ref[:, sl] = (y_ref[o].astype(F32) * scale * gain_ref[:, sl]).astype(BF16)


VM = pl.BlockSpec(memory_space=pltpu.VMEM)
SM = pl.BlockSpec(memory_space=pltpu.SMEM)
HB = pl.BlockSpec(memory_space=pl.ANY)


def kept(x):
    return pltpu.with_memory_space_constraint(x, pltpu.VMEM)


def far(x):
    return pltpu.with_memory_space_constraint(x, pltpu.HBM)


def call(kernel, specs, outs, *args, scratch=()):
    return pl.pallas_call(
        kernel,
        in_specs=specs,
        out_specs=[VM] * len(outs),
        out_shape=outs,
        scratch_shapes=list(scratch),
        compiler_params=pltpu.CompilerParams(vmem_limit_bytes=14 << 20),
    )(*args)


def whole(tokens, bc_proj, step_sizes, decay_rates, direct_weight, norm_gain, routes, segments):
    V = pltpu.VMEM
    send, send_c = call(
        pack_kernel,
        [HB] * 5,
        [V((PEERS, TOK + AUX, 2 * WIDE), BF16), V((PEERS, TOK, WIDE), BF16)],
        far(tokens[0]), far(bc_proj[0]), far(step_sizes[0]), far(routes.reshape(1, 16)), far(segments),
        scratch=[
            V((TOK, 2, 2 * WIDE), BF16),
            V((16, 256), BF16),
            V((1, 16), jnp.int32),
            V((1, 256), jnp.int32),
            pltpu.SemaphoreType.DMA((4 + PEERS,)),
        ],
    )
    got = kept(lax.all_to_all(send, ("dp", "y"), split_axis=0, concat_axis=0, tiled=True))
    got_c = kept(lax.all_to_all(send_c, ("dp", "y"), split_axis=0, concat_axis=0, tiled=True))
    e, f, xs = call(
        state_kernel,
        [SM, VM],
        [pltpu.HBM((2, WIDE + AUX, WIDE), BF16), V((SPAN, WIDE), F32), V((SPAN, WIDE), BF16)],
        decay_rates, got,
        scratch=[V((SPAN, SPAN), BF16), V((SPAN, WIDE), BF16), V((2, SPAN, WIDE), BF16)],
    )
    f, xs = kept(f), kept(xs)
    e2 = kept(lax.ppermute(e, "z", [(i, i + 2) for i in range(2)]))
    e1 = kept(lax.ppermute(e, "z", [(i, i + 1) for i in range(3)]))
    base, cm, meta = call(
        inside_kernel,
        [SM] + [VM] * 4,
        [V((SPAN, WIDE), F32), V((SPAN, 2 * WIDE), BF16), V((AUX, TOK), F32)],
        direct_weight, got, got_c, f, xs,
        scratch=[V((SPAN, WIDE), BF16), V((SPAN, WIDE), BF16)],
    )
    (out,) = call(
        carry_kernel,
        [VM] * 6,
        [V((PEERS, TOK, WIDE), BF16)],
        kept(base), f, kept(cm), e1, e2, kept(meta),
        scratch=[V((2 * WIDE, WIDE), BF16)],
    )
    back = kept(lax.all_to_all(out, ("dp", "y"), split_axis=0, concat_axis=0, tiled=True))
    (s0,) = call(square_kernel, [VM], [V((AUX, TOK), F32)], back)
    others = [kept(lax.ppermute(s0, "tensor", [(i, (i + k) % 4) for i in range(4)])) for k in (1, 2, 3)]

    def scale(*refs):
        scale_kernel(*refs, features=128 * 64)

    out_shape = [jax.ShapeDtypeStruct((TOK, PEERS * WIDE), BF16)]
    (mixed,) = call(scale, [VM] * 6, out_shape, back, kept(s0), *others, norm_gain[None])
    return mixed[None]


def solution(mesh):
    fine = Mesh(mesh.devices.reshape(2, 4, 4, 4), ("dp", "z", "y", "tensor"))
    rows = ("z", "y")
    return jax.shard_map(
        whole,
        mesh=fine,
        in_specs=(
            P("dp", rows, "tensor"),
            P("dp", rows, None, "tensor"),
            P("dp", rows, "tensor"),
            P("tensor"),
            P("tensor"),
            P("tensor"),
            P("dp", rows, None),
            P("dp", rows),
        ),
        out_specs=P("dp", rows, "tensor"),
        check_vma=False,
    )
```

profile of v0, /device:TPU:64, one launch (start us, length us, event | category | flops | bytes accessed | tf_op | source)
XLA Modules:
  0.0 72.5 jit_solution(186850499878725356)
XLA Ops:
  0.0 2.5 %shard_map.82 = (bf16[8,136,512]{2,1,0:T(8,128)(2,1)S(1)}, bf16[8,128,256]{2,1,0:T(8,128)(2,1)}) custom-call(bf16[128,2048]{1,0:T(8,128)(2,1)} %bitcast.7, bf16[128,2,512]{2,1,0:T(2,128)(2,1)} %bitcast.8, bf16[16,256]{1,0:T(8,128)(2,1)} %bitcast.9, s32[1,16]{1,0:T(1,128)} %bitcast.10, s32[1,256]{1,0:T(1,128)} %seg_ref.1), custom_call_target="tpu_custom_call" | custom-call | tf_op jit(solution)/shard_map/pallas_call | solution.py:237
  2.5 0.0 copy-start.1
  2.5 21.9 %all_to_all.15.r_ref = bf16[8,136,512]{2,1,0:T(8,128)(2,1)S(1)} all-to-all(bf16[8,136,512]{2,1,0:T(8,128)(2,1)S(1)} %get-tuple-element.13), channel_id=1, replica_groups=mesh['dp'=2,'z'=4,'y'=4,'tensor'=4] {'dp','y'}, dimensions={0} | all-to-all | bytes 2228224 | tf_op jit(solution)/shard_map/all_to_all | solution.py:262
  24.4 0.0 copy-start.2
  24.4 3.6 %all-to-all-start.1 = ((bf16[8,128,256]{2,1,0:T(8,128)(2,1)}), bf16[8,128,256]{2,1,0:T(8,128)(2,1)S(1)}, u32[]{:S(2)}, u32[]{:S(2)}) async-start(bf16[8,128,256]{2,1,0:T(8,128)(2,1)} %get-tuple-element.14), calls=%async_computation.1 | async-start | bytes 1048576 | tf_op jit(solution)/shard_map/all_to_all | solution.py:263
  28.0 0.0 copy-done.1
  28.0 3.4 %shard_map.83 = (bf16[2,264,256]{2,1,0:T(8,128)(2,1)}, f32[1024,256]{1,0:T(8,128)S(1)}, bf16[1024,256]{1,0:T(8,128)(2,1)S(1)}) custom-call(f32[32]{0:T(128)S(1)} %copy-done.1, bf16[8,136,512]{2,1,0:T(8,128)(2,1)S(1)} %all_to_all.15.r_ref), custom_call_target="tpu_custom_call" | custom-call | tf_op jit(solution)/shard_map/pallas_call | solution.py:237
  31.5 1.3 %collective-permute-start.1 = (bf16[2,264,256]{2,1,0:T(8,128)(2,1)}, bf16[2,264,256]{2,1,0:T(8,128)(2,1)S(1)}, u32[]{:S(2)}, u32[]{:S(2)}) collective-permute-start(bf16[2,264,256]{2,1,0:T(8,128)(2,1)} %get-tuple-element.19), channel_id=1, source_target_pairs={{0,32},{16,48},{1,33},{17,49},{2,34},{18,50},{3,35},{19,51},{4,36}... | collective-permute-start | bytes 811016 | tf_op jit(solution)/shard_map/ppermute | solution.py:272
  32.8 3.5 %collective-permute-start = (bf16[2,264,256]{2,1,0:T(8,128)(2,1)}, bf16[2,264,256]{2,1,0:T(8,128)(2,1)}, u32[]{:S(2)}, u32[]{:S(2)}) collective-permute-start(bf16[2,264,256]{2,1,0:T(8,128)(2,1)} %get-tuple-element.19), channel_id=1, source_target_pairs={{0,16},{16,32},{32,48},{1,17},{17,33},{33,49},{2,18},{18,34},{34,5... | collective-permute-start | bytes 811016 | tf_op jit(solution)/shard_map/ppermute | solution.py:273
  36.3 0.0 all-to-all-done.1.got_ref
  36.3 0.0 copy-done.2
  36.3 2.0 %shard_map.84 = (f32[1024,256]{1,0:T(8,128)S(1)}, bf16[1024,512]{1,0:T(8,128)(2,1)S(1)}, f32[8,128]{1,0:T(8,128)S(1)}) custom-call(f32[32]{0:T(128)S(1)} %copy-done.2, bf16[8,136,512]{2,1,0:T(8,128)(2,1)S(1)} %all_to_all.15.r_ref, bf16[8,128,256]{2,1,0:T(8,128)(2,1)S(1)} %all-to-all-done.1.got_ref, f32[1024,256]{1,0:T(8,128)S(1)} %get-tuple-element.15.f_ref, ...), custom_call_target="tpu_custom_call" | custom-call | tf_op jit(solution)/shard_map/pallas_call | solution.py:237
  38.3 6.1 %collective-permute-done.1.e2_ref = bf16[2,264,256]{2,1,0:T(8,128)(2,1)S(1)} collective-permute-done((bf16[2,264,256]{2,1,0:T(8,128)(2,1)}, bf16[2,264,256]{2,1,0:T(8,128)(2,1)S(1)}, u32[]{:S(2)}, u32[]{:S(2)}) %collective-permute-start.1) | collective-permute-done | bytes 270368 | tf_op jit(solution)/shard_map/ppermute | solution.py:272
  44.4 3.1 %collective-permute-done.e1_ref = bf16[2,264,256]{2,1,0:T(8,128)(2,1)} collective-permute-done((bf16[2,264,256]{2,1,0:T(8,128)(2,1)}, bf16[2,264,256]{2,1,0:T(8,128)(2,1)}, u32[]{:S(2)}, u32[]{:S(2)}) %collective-permute-start) | collective-permute-done | bytes 270368 | tf_op jit(solution)/shard_map/ppermute | solution.py:273
  47.6 1.5 %shard_map.85 = bf16[8,128,256]{2,1,0:T(8,128)(2,1)S(1)} custom-call(f32[1024,256]{1,0:T(8,128)S(1)} %get-tuple-element.17.base_ref, f32[1024,256]{1,0:T(8,128)S(1)} %get-tuple-element.15.f_ref, bf16[1024,512]{1,0:T(8,128)(2,1)S(1)} %get-tuple-element.18.cm_ref, bf16[2,264,256]{2,1,0:T(8,128)(2,1)} %collective-permute-done.e1_ref, ...), custom_call_target="tpu_custom_call" | custom-call | tf_op jit(solution)/shard_map/pallas_call | solution.py:237
  49.1 0.0 copy-start
  49.1 14.6 %all_to_all.16.y_ref.refs_0_ = bf16[8,128,256]{2,1,0:T(8,128)(2,1)S(1)} all-to-all(bf16[8,128,256]{2,1,0:T(8,128)(2,1)S(1)} %shard_map.85), channel_id=1, replica_groups=mesh['dp'=2,'z'=4,'y'=4,'tensor'=4] {'dp','y'}, dimensions={0} | all-to-all | bytes 1048576 | tf_op jit(solution)/shard_map/all_to_all | solution.py:288
  63.7 0.3 shard_map.86.refs_1_
  64.0 0.0 collective-permute-start.4
  64.0 2.8 %collective-permute-start.3 = (f32[8,128]{1,0:T(8,128)S(1)}, f32[8,128]{1,0:T(8,128)S(1)}, u32[]{:S(2)}, u32[]{:S(2)}) collective-permute-start(f32[8,128]{1,0:T(8,128)S(1)} %shard_map.86.refs_1_), channel_id=1, source_target_pairs={{0,2},{1,3},{2,0},{3,1},{4,6},{5,7},{6,4},{7,5},{8,10},{9,11},{10,... | collective-permute-start | bytes 12296 | tf_op jit(solution)/shard_map/ppermute | solution.py:290
  66.8 0.2 collective-permute-start.2
  67.0 0.0 collective-permute-done.4.refs_4_
  67.0 2.2 %collective-permute-done.3.refs_3_ = f32[8,128]{1,0:T(8,128)S(1)} collective-permute-done((f32[8,128]{1,0:T(8,128)S(1)}, f32[8,128]{1,0:T(8,128)S(1)}, u32[]{:S(2)}, u32[]{:S(2)}) %collective-permute-start.3) | collective-permute-done | bytes 4128 | tf_op jit(solution)/shard_map/ppermute | solution.py:290
  69.1 2.1 %collective-permute-done.2.refs_2_ = f32[8,128]{1,0:T(8,128)S(1)} collective-permute-done((f32[8,128]{1,0:T(8,128)S(1)}, f32[8,128]{1,0:T(8,128)S(1)}, u32[]{:S(2)}, u32[]{:S(2)}) %collective-permute-start.2) | collective-permute-done | bytes 4128 | tf_op jit(solution)/shard_map/ppermute | solution.py:290
  71.3 0.0 copy-done
  71.3 1.2 %shard_map.87 = bf16[128,2048]{1,0:T(8,128)(2,1)} custom-call(bf16[8,128,256]{2,1,0:T(8,128)(2,1)S(1)} %all_to_all.16.y_ref.refs_0_, f32[8,128]{1,0:T(8,128)S(1)} %shard_map.86.refs_1_, f32[8,128]{1,0:T(8,128)S(1)} %collective-permute-done.2.refs_2_, f32[8,128]{1,0:T(8,128)S(1)} %collective-permute-done.3.refs_3_, ...), custom_call_target="tpu_custom_call" | custom-call | tf_op jit(solution)/shard_map/pallas_call | solution.py:237
Async XLA Ops:
  2.5 25.5 %copy-start.1 = (f32[32]{0:T(128)S(1)}, f32[32]{0:T(128)}, u32[]{:S(2)}) copy-start(f32[32]{0:T(128)} %rate_ref.1) | copy-start | bytes 388
  24.4 11.9 %copy-start.2 = (f32[32]{0:T(128)S(1)}, f32[32]{0:T(128)}, u32[]{:S(2)}) copy-start(f32[32]{0:T(128)} %weight_ref.1) | copy-start | bytes 388
  24.4 11.9 %all-to-all-start.1 = ((bf16[8,128,256]{2,1,0:T(8,128)(2,1)}), bf16[8,128,256]{2,1,0:T(8,128)(2,1)S(1)}, u32[]{:S(2)}, u32[]{:S(2)}) async-start(bf16[8,128,256]{2,1,0:T(8,128)(2,1)} %get-tuple-element.14), calls=%async_computation.1 | async-start | bytes 1048576 | tf_op jit(solution)/shard_map/all_to_all | solution.py:263
  31.5 13.0 %collective-permute-start.1 = (bf16[2,264,256]{2,1,0:T(8,128)(2,1)}, bf16[2,264,256]{2,1,0:T(8,128)(2,1)S(1)}, u32[]{:S(2)}, u32[]{:S(2)}) collective-permute-start(bf16[2,264,256]{2,1,0:T(8,128)(2,1)} %get-tuple-element.19), channel_id=1, source_target_pairs={{0,32},{16,48},{1,33},{17,49},{2,34},{18,50},{3,35},{19,51},{4,36}... | collective-permute-start | bytes 811016 | tf_op jit(solution)/shard_map/ppermute | solution.py:272
  32.8 14.8 %collective-permute-start = (bf16[2,264,256]{2,1,0:T(8,128)(2,1)}, bf16[2,264,256]{2,1,0:T(8,128)(2,1)}, u32[]{:S(2)}, u32[]{:S(2)}) collective-permute-start(bf16[2,264,256]{2,1,0:T(8,128)(2,1)} %get-tuple-element.19), channel_id=1, source_target_pairs={{0,16},{16,32},{32,48},{1,17},{17,33},{33,49},{2,18},{18,34},{34,5... | collective-permute-start | bytes 811016 | tf_op jit(solution)/shard_map/ppermute | solution.py:273
  49.1 22.2 %copy-start = (f32[2048]{0:T(1024)S(1)}, f32[2048]{0:T(1024)}, u32[]{:S(2)}) copy-start(f32[2048]{0:T(1024)} %param.13) | copy-start | bytes 24580
  64.0 3.0 %collective-permute-start.4 = (f32[8,128]{1,0:T(8,128)S(1)}, f32[8,128]{1,0:T(8,128)S(1)}, u32[]{:S(2)}, u32[]{:S(2)}) collective-permute-start(f32[8,128]{1,0:T(8,128)S(1)} %shard_map.86.refs_1_), channel_id=1, source_target_pairs={{0,3},{1,0},{2,1},{3,2},{4,7},{5,4},{6,5},{7,6},{8,11},{9,8},{10,9... | collective-permute-start | bytes 12296 | tf_op jit(solution)/shard_map/ppermute | solution.py:290
  64.0 5.2 %collective-permute-start.3 = (f32[8,128]{1,0:T(8,128)S(1)}, f32[8,128]{1,0:T(8,128)S(1)}, u32[]{:S(2)}, u32[]{:S(2)}) collective-permute-start(f32[8,128]{1,0:T(8,128)S(1)} %shard_map.86.refs_1_), channel_id=1, source_target_pairs={{0,2},{1,3},{2,0},{3,1},{4,6},{5,7},{6,4},{7,5},{8,10},{9,11},{10,... | collective-permute-start | bytes 12296 | tf_op jit(solution)/shard_map/ppermute | solution.py:290
  66.8 4.5 %collective-permute-start.2 = (f32[8,128]{1,0:T(8,128)S(1)}, f32[8,128]{1,0:T(8,128)S(1)}, u32[]{:S(2)}, u32[]{:S(2)}) collective-permute-start(f32[8,128]{1,0:T(8,128)S(1)} %shard_map.86.refs_1_), channel_id=1, source_target_pairs={{0,1},{1,2},{2,3},{3,0},{4,5},{5,6},{6,7},{7,4},{8,9},{9,10},{10,1... | collective-permute-start | bytes 12296 | tf_op jit(solution)/shard_map/ppermute | solution.py:290
where the time goes:
time: 72.8 us; the launch traced here: 72.5 us
  blocking collectives  36.4 us (50%)
  waiting for transfers between devices  13.6 us (19%)
  starting transfers between devices  11.4 us (16%)
  Pallas kernels  10.9 us (15%)
    all_to_all x1, blocking collectives, whole(): lax.all_to_all(send, ('dp', 'y'), split_axis=0, concat_axis=0, tiled=True)  21.9 us
    all_to_all x1, blocking collectives, whole(): lax.all_to_all(out, ('dp', 'y'), split_axis=0, concat_axis=0, tiled=True)  14.6 us
    pallas_call x6, Pallas kernels, call(): pl.pallas_call(kernel, in_specs=specs, out_specs=[VM] * len(outs), out_sh...  10.9 us
    ppermute x1, waiting for transfers between devices, whole(): e2 = kept(lax.ppermute(e, 'z', [(i, i + 2) for i in range(2)]))  6.13 us
    ppermute x3, waiting for transfers between devices, whole(): lax.ppermute(s0, 'tensor', [(i, (i + k) % 4) for i in range(4)])  4.33 us
    all_to_all x1, starting transfers between devices, whole(): lax.all_to_all(send_c, ('dp', 'y'), split_axis=0, concat_axis=0, tiled=True)  3.63 us
    ppermute x1, starting transfers between devices, whole(): e1 = kept(lax.ppermute(e, 'z', [(i, i + 1) for i in range(3)]))  3.53 us
    ppermute x1, waiting for transfers between devices, whole(): e1 = kept(lax.ppermute(e, 'z', [(i, i + 1) for i in range(3)]))  3.15 us
  transfers between devices with their start and end apart: 6, of which 4 were waited for; matrix products, arithmetic and copies ran while one was open for 0% of the time, Pallas kernels for 7%

commit v1 on v0

--- a/solution.py
+++ b/solution.py
@@ -112,10 +112,10 @@
     return [key_of(*p) for p in rows], [key_of(*p) for p in cols], first, last
 
 
-def state_kernel(rate_ref, r_ref, e_ref, f_ref, xs_ref, m_ref, dt_ref, bm_ref):
+def state_kernel(rate_ref, r_ref, e_ref, f_ref, xs_ref, own_ref, m_ref, dt_ref, bm_ref):
     rate = rate_lanes(rate_ref)
     spread = ones_where(iota((AUX, WIDE), 1) // 64 == iota((AUX, WIDE), 0), BF16)
-    key_rows, key_cols, _, last = keys_of(r_ref)
+    key_rows, key_cols, first, last = keys_of(r_ref)
     causal = iota((TOK, TOK), 0) >= iota((TOK, TOK), 1)
     for i in range(PEERS):
         src = (i % 2) * 4 + i // 2
@@ -151,13 +151,13 @@
         through = jnp.exp(-rate * total)
         e = dot(bm_ref[d], xs_ref[...], ((0,), (0,))) * through[0:1]
         e_ref[d, 0:WIDE, :] = e.astype(BF16)
-        e_ref[d, WIDE : WIDE + AUX, :] = jnp.where(row8 == 0, through, last[d]).astype(BF16)
-
-
-def inside_kernel(weight_ref, r_ref, got_ref, f_ref, xs_ref, base_ref, cm_ref, meta_ref, b_ref, c_ref):
+        e_ref[d, WIDE : WIDE + AUX, :] = jnp.broadcast_to(last[d], (AUX, WIDE)).astype(BF16)
+        own_ref[d] = jnp.where(row8 == 0, jnp.where(first[d] == last[d], through, 0.0), first[d])
+
+
+def inside_kernel(weight_ref, r_ref, got_ref, f_ref, xs_ref, base_ref, cm_ref, b_ref, c_ref):
     weight = rate_lanes(weight_ref)
     key_rows, key_cols, first, _ = keys_of(r_ref)
-    meta_ref[...] = jnp.where(iota((AUX, TOK), 0) == 0, first[0], first[1])
     for q in range(PEERS):
         src = (q % 2) * 4 + q // 2
         sl = slice(q * TOK, (q + 1) * TOK)
@@ -187,14 +187,18 @@
             base_ref[at : at + TOK, :] = acc[s * TOK : (s + 1) * TOK] + weight * x
 
 
-def carry_kernel(base_ref, f_ref, cm_ref, e1_ref, e2_ref, meta_ref, y_ref, h_ref):
+def pass_kernel(e_ref, own_ref, out_ref):
     for d in range(2):
-        first = meta_ref[d : d + 1, 0:1]
-        joined1 = e1_ref[d, WIDE + 1 : WIDE + 2, :].astype(F32) == first
-        joined2 = joined1 & (e2_ref[d, WIDE + 1 : WIDE + 2, :].astype(F32) == first)
-        through = jnp.where(joined2, e1_ref[d, WIDE : WIDE + 1, :].astype(F32), 0.0)
-        near = jnp.where(joined1, e1_ref[d, 0:WIDE, :].astype(F32), 0.0)
-        h_ref[d * WIDE : (d + 1) * WIDE, :] = (near + through * e2_ref[d, 0:WIDE, :].astype(F32)).astype(BF16)
+        joined = e_ref[d, WIDE : WIDE + 1, :].astype(F32) == own_ref[d, 1:2, :]
+        through = jnp.where(joined, own_ref[d, 0:1, :], 0.0)
+        out_ref[d] = (through * e_ref[d, 0:WIDE, :].astype(F32)).astype(BF16)
+
+
+def carry_kernel(base_ref, f_ref, cm_ref, e1_ref, e2_ref, own_ref, y_ref, h_ref):
+    for d in range(2):
+        joined = e1_ref[d, WIDE : WIDE + 1, :].astype(F32) == own_ref[d, 1:2, :]
+        h = e1_ref[d, 0:WIDE, :].astype(F32) + e2_ref[d].astype(F32)
+        h_ref[d * WIDE : (d + 1) * WIDE, :] = jnp.where(joined, h, 0.0).astype(BF16)
     for q in range(PEERS):
         sl = slice(q * TOK, (q + 1) * TOK)
         y = base_ref[sl, :] + f_ref[sl, :] * dot(cm_ref[sl, :], h_ref[...], ((1,), (0,)))
@@ -249,7 +253,7 @@
     send, send_c = call(
         pack_kernel,
         [HB] * 5,
-        [V((PEERS, TOK + AUX, 2 * WIDE), BF16), V((PEERS, TOK, WIDE), BF16)],
+        [V((PEERS, TOK + AUX, 2 * WIDE), BF16), pltpu.HBM((PEERS, TOK, WIDE), BF16)],
         far(tokens[0]), far(bc_proj[0]), far(step_sizes[0]), far(routes.reshape(1, 16)), far(segments),
         scratch=[
             V((TOK, 2, 2 * WIDE), BF16),
@@ -260,21 +264,23 @@
         ],
     )
     got = kept(lax.all_to_all(send, ("dp", "y"), split_axis=0, concat_axis=0, tiled=True))
-    got_c = kept(lax.all_to_all(send_c, ("dp", "y"), split_axis=0, concat_axis=0, tiled=True))
-    e, f, xs = call(
+    e, f, xs, own = call(
         state_kernel,
         [SM, VM],
-        [pltpu.HBM((2, WIDE + AUX, WIDE), BF16), V((SPAN, WIDE), F32), V((SPAN, WIDE), BF16)],
+        [pltpu.HBM((2, WIDE + AUX, WIDE), BF16), V((SPAN, WIDE), F32), V((SPAN, WIDE), BF16), V((2, AUX, WIDE), F32)],
         decay_rates, got,
         scratch=[V((SPAN, SPAN), BF16), V((SPAN, WIDE), BF16), V((2, SPAN, WIDE), BF16)],
     )
-    f, xs = kept(f), kept(xs)
-    e2 = kept(lax.ppermute(e, "z", [(i, i + 2) for i in range(2)]))
+    f, xs, own = kept(f), kept(xs), kept(own)
+    e, send_c = lax.optimization_barrier((e, send_c))
     e1 = kept(lax.ppermute(e, "z", [(i, i + 1) for i in range(3)]))
-    base, cm, meta = call(
+    got_c = kept(lax.all_to_all(send_c, ("dp", "y"), split_axis=0, concat_axis=0, tiled=True))
+    (older,) = call(pass_kernel, [VM, VM], [pltpu.HBM((2, WIDE, WIDE), BF16)], e1, own)
+    e2 = kept(lax.ppermute(older, "z", [(i, i + 1) for i in range(1, 3)]))
+    base, cm = call(
         inside_kernel,
         [SM] + [VM] * 4,
-        [V((SPAN, WIDE), F32), V((SPAN, 2 * WIDE), BF16), V((AUX, TOK), F32)],
+        [V((SPAN, WIDE), F32), V((SPAN, 2 * WIDE), BF16)],
         direct_weight, got, got_c, f, xs,
         scratch=[V((SPAN, WIDE), BF16), V((SPAN, WIDE), BF16)],
     )
@@ -282,7 +288,7 @@
         carry_kernel,
         [VM] * 6,
         [V((PEERS, TOK, WIDE), BF16)],
-        kept(base), f, kept(cm), e1, e2, kept(meta),
+        kept(base), f, kept(cm), e1, e2, own,
         scratch=[V((2 * WIDE, WIDE), BF16)],
     )
     back = kept(lax.all_to_all(out, ("dp", "y"), split_axis=0, concat_axis=0, tiled=True))

time: 72.8 us -> 68.8 us (0.945)
  waiting for transfers between devices: 13.6 us -> 9 us
  blocking collectives: 36.4 us -> 34.3 us
  starting transfers between devices: 11.4 us -> 13.5 us
    ppermute x1, waiting for transfers between devices: 6.13 us -> 0.74 us  [whole(): e2 = kept(lax.ppermute(older, 'z', [(i, i + 1) for i in range(1, 3)]))]
    all_to_all x1, waiting for transfers between devices: 0.01 us -> 2.27 us  [whole(): lax.all_to_all(send_c, ('dp', 'y'), split_axis=0, concat_axis=0, tiled=True)]
    ppermute x1, starting transfers between devices: 1.28 us -> 3.52 us  [whole(): e2 = kept(lax.ppermute(older, 'z', [(i, i + 1) for i in range(1, 3)]))]
    all_to_all x1, blocking collectives: 14.6 us -> 12.4 us  [whole(): lax.all_to_all(out, ('dp', 'y'), split_axis=0, concat_axis=0, tiled=True)]
    ppermute x1, waiting for transfers between devices: 3.15 us -> 1.66 us  [whole(): e1 = kept(lax.ppermute(e, 'z', [(i, i + 1) for i in range(3)]))]
    pallas_call x6 -> x7, Pallas kernels: 10.9 us -> 11.6 us  [call(): pl.pallas_call(kernel, in_specs=specs, out_specs=[VM] * len(outs), out_sh...]
  transfers between devices with their start and end apart: 6 -> 6, of which waited for: 4 -> 5; matrix products, arithmetic and copies ran while one was open for 0% -> 0% of each run, Pallas kernels for 7% -> 4%
where the time goes in v1:
time: 68.8 us; the launch traced here: 68.4 us
  blocking collectives  34.3 us (50%)
  starting transfers between devices  13.5 us (20%)
  Pallas kernels  11.6 us (17%)
  waiting for transfers between devices  9 us (13%)
    all_to_all x1, blocking collectives, whole(): lax.all_to_all(send, ('dp', 'y'), split_axis=0, concat_axis=0, tiled=True)  21.9 us
    all_to_all x1, blocking collectives, whole(): lax.all_to_all(out, ('dp', 'y'), split_axis=0, concat_axis=0, tiled=True)  12.4 us
    pallas_call x7, Pallas kernels, call(): pl.pallas_call(kernel, in_specs=specs, out_specs=[VM] * len(outs), out_sh...  11.6 us
    ppermute x3, waiting for transfers between devices, whole(): lax.ppermute(s0, 'tensor', [(i, (i + k) % 4) for i in range(4)])  4.33 us
    ppermute x1, starting transfers between devices, whole(): e1 = kept(lax.ppermute(e, 'z', [(i, i + 1) for i in range(3)]))  3.52 us
    ppermute x1, starting transfers between devices, whole(): e2 = kept(lax.ppermute(older, 'z', [(i, i + 1) for i in range(1, 3)]))  3.52 us
    all_to_all x1, starting transfers between devices, whole(): lax.all_to_all(send_c, ('dp', 'y'), split_axis=0, concat_axis=0, tiled=True)  3.51 us
    ppermute x3, starting transfers between devices, whole(): lax.ppermute(s0, 'tensor', [(i, (i + k) % 4) for i in range(4)])  2.99 us
  transfers between devices with their start and end apart: 6, of which 5 were waited for; matrix products, arithmetic and copies ran while one was open for 0% of the time, Pallas kernels for 4%

profile of v1, /device:TPU:64, one launch (start us, length us, event | category | flops | bytes accessed | tf_op | source)
XLA Modules:
  0.0 68.4 jit_solution(12467184344277492856)
XLA Ops:
  0.0 2.5 %shard_map.82 = (bf16[8,136,512]{2,1,0:T(8,128)(2,1)S(1)}, bf16[8,128,256]{2,1,0:T(8,128)(2,1)}) custom-call(bf16[128,2048]{1,0:T(8,128)(2,1)} %bitcast.7, bf16[128,2,512]{2,1,0:T(2,128)(2,1)} %bitcast.8, bf16[16,256]{1,0:T(8,128)(2,1)} %bitcast.9, s32[1,16]{1,0:T(1,128)} %bitcast.10, s32[1,256]{1,0:T(1,128)} %seg_ref.1), custom_call_target="tpu_custom_call" | custom-call | tf_op jit(solution)/shard_map/pallas_call | solution.py:241
  2.5 0.0 copy-start.1
  2.5 21.9 %all_to_all.15.r_ref = bf16[8,136,512]{2,1,0:T(8,128)(2,1)S(1)} all-to-all(bf16[8,136,512]{2,1,0:T(8,128)(2,1)S(1)} %get-tuple-element.15), channel_id=1, replica_groups=mesh['dp'=2,'z'=4,'y'=4,'tensor'=4] {'dp','y'}, dimensions={0} | all-to-all | bytes 2228224 | tf_op jit(solution)/shard_map/all_to_all | solution.py:266
  24.4 0.0 copy-done.1
  24.4 0.0 copy-start.2
  24.4 3.4 %shard_map.83 = (bf16[2,264,256]{2,1,0:T(8,128)(2,1)}, f32[1024,256]{1,0:T(8,128)S(1)}, bf16[1024,256]{1,0:T(8,128)(2,1)S(1)}, f32[2,8,256]{2,1,0:T(8,128)S(1)}) custom-call(f32[32]{0:T(128)S(1)} %copy-done.1, bf16[8,136,512]{2,1,0:T(8,128)(2,1)S(1)} %all_to_all.15.r_ref), custom_call_target="tpu_custom_call" | custom-call | tf_op jit(solution)/shard_map/pallas_call | solution.py:241
  27.8 3.5 %collective-permute-start = (bf16[2,264,256]{2,1,0:T(8,128)(2,1)}, bf16[2,264,256]{2,1,0:T(8,128)(2,1)S(1)}, u32[]{:S(2)}, u32[]{:S(2)}) collective-permute-start(bf16[2,264,256]{2,1,0:T(8,128)(2,1)} %get-tuple-element.23), channel_id=1, source_target_pairs={{0,16},{16,32},{32,48},{1,17},{17,33},{33,49},{2,18},{18,34},{34,5... | collective-permute-start | bytes 811016 | tf_op jit(solution)/shard_map/ppermute | solution.py:276
  31.4 3.5 %all-to-all-start.1 = ((bf16[8,128,256]{2,1,0:T(8,128)(2,1)}), bf16[8,128,256]{2,1,0:T(8,128)(2,1)S(1)}, u32[]{:S(2)}, u32[]{:S(2)}) async-start(bf16[8,128,256]{2,1,0:T(8,128)(2,1)} %get-tuple-element.18), calls=%async_computation.1 | async-start | bytes 1048576 | tf_op jit(solution)/shard_map/all_to_all | solution.py:277
  34.9 1.7 %collective-permute-done.e_ref.e1_ref = bf16[2,264,256]{2,1,0:T(8,128)(2,1)S(1)} collective-permute-done((bf16[2,264,256]{2,1,0:T(8,128)(2,1)}, bf16[2,264,256]{2,1,0:T(8,128)(2,1)S(1)}, u32[]{:S(2)}, u32[]{:S(2)}) %collective-permute-start) | collective-permute-done | bytes 270368 | tf_op jit(solution)/shard_map/ppermute | solution.py:276
  36.5 0.8 %shard_map.85 = bf16[2,256,256]{2,1,0:T(8,128)(2,1)} custom-call(bf16[2,264,256]{2,1,0:T(8,128)(2,1)S(1)} %collective-permute-done.e_ref.e1_ref, f32[2,8,256]{2,1,0:T(8,128)S(1)} %get-tuple-element.24.own_ref), custom_call_target="tpu_custom_call" | custom-call | tf_op jit(solution)/shard_map/pallas_call | solution.py:241
  37.3 3.5 %collective-permute-start.1 = (bf16[2,256,256]{2,1,0:T(8,128)(2,1)}, bf16[2,256,256]{2,1,0:T(8,128)(2,1)}, u32[]{:S(2)}, u32[]{:S(2)}) collective-permute-start(bf16[2,256,256]{2,1,0:T(8,128)(2,1)} %shard_map.85), channel_id=1, source_target_pairs={{16,32},{32,48},{17,33},{33,49},{18,34},{34,50},{19,35},{35,51},{2... | collective-permute-start | bytes 786440 | tf_op jit(solution)/shard_map/ppermute | solution.py:279
  40.8 2.3 %all-to-all-done.1.got_ref = bf16[8,128,256]{2,1,0:T(8,128)(2,1)S(1)} async-done(((bf16[8,128,256]{2,1,0:T(8,128)(2,1)}), bf16[8,128,256]{2,1,0:T(8,128)(2,1)S(1)}, u32[]{:S(2)}, u32[]{:S(2)}) %all-to-all-start.1) | async-done | bytes 524320 | tf_op jit(solution)/shard_map/all_to_all | solution.py:277
  43.1 0.0 copy-done.2
  43.1 2.0 %shard_map.84 = (f32[1024,256]{1,0:T(8,128)S(1)}, bf16[1024,512]{1,0:T(8,128)(2,1)S(1)}) custom-call(f32[32]{0:T(128)S(1)} %copy-done.2, bf16[8,136,512]{2,1,0:T(8,128)(2,1)S(1)} %all_to_all.15.r_ref, bf16[8,128,256]{2,1,0:T(8,128)(2,1)S(1)} %all-to-all-done.1.got_ref, f32[1024,256]{1,0:T(8,128)S(1)} %get-tuple-element.19.f_ref, ...), custom_call_target="tpu_custom_call" | custom-call | tf_op jit(solution)/shard_map/pallas_call | solution.py:241
  45.1 0.7 %collective-permute-done.1.e2_ref = bf16[2,256,256]{2,1,0:T(8,128)(2,1)} collective-permute-done((bf16[2,256,256]{2,1,0:T(8,128)(2,1)}, bf16[2,256,256]{2,1,0:T(8,128)(2,1)}, u32[]{:S(2)}, u32[]{:S(2)}) %collective-permute-start.1) | collective-permute-done | bytes 262176 | tf_op jit(solution)/shard_map/ppermute | solution.py:279
  45.9 1.4 %shard_map.86 = bf16[8,128,256]{2,1,0:T(8,128)(2,1)S(1)} custom-call(f32[1024,256]{1,0:T(8,128)S(1)} %get-tuple-element.21.base_ref, f32[1024,256]{1,0:T(8,128)S(1)} %get-tuple-element.19.f_ref, bf16[1024,512]{1,0:T(8,128)(2,1)S(1)} %get-tuple-element.22.cm_ref, bf16[2,264,256]{2,1,0:T(8,128)(2,1)S(1)} %collective-permute-done.e_ref.e1_ref, ...), custom_call_target="tpu_custom_call" | custom-call | tf_op jit(solution)/shard_map/pallas_call | solution.py:241
  47.3 0.0 copy-start
  47.3 12.4 %all_to_all.16.y_ref.refs_0_ = bf16[8,128,256]{2,1,0:T(8,128)(2,1)S(1)} all-to-all(bf16[8,128,256]{2,1,0:T(8,128)(2,1)S(1)} %shard_map.86), channel_id=1, replica_groups=mesh['dp'=2,'z'=4,'y'=4,'tensor'=4] {'dp','y'}, dimensions={0} | all-to-all | bytes 1048576 | tf_op jit(solution)/shard_map/all_to_all | solution.py:294
  59.7 0.3 shard_map.87.refs_1_
  59.9 0.0 collective-permute-start.4
  59.9 2.8 %collective-permute-start.3 = (f32[8,128]{1,0:T(8,128)S(1)}, f32[8,128]{1,0:T(8,128)S(1)}, u32[]{:S(2)}, u32[]{:S(2)}) collective-permute-start(f32[8,128]{1,0:T(8,128)S(1)} %shard_map.87.refs_1_), channel_id=1, source_target_pairs={{0,2},{1,3},{2,0},{3,1},{4,6},{5,7},{6,4},{7,5},{8,10},{9,11},{10,... | collective-permute-start | bytes 12296 | tf_op jit(solution)/shard_map/ppermute | solution.py:296
  62.7 0.2 collective-permute-start.2
  62.9 0.0 collective-permute-done.4.refs_4_
  62.9 2.2 %collective-permute-done.3.refs_3_ = f32[8,128]{1,0:T(8,128)S(1)} collective-permute-done((f32[8,128]{1,0:T(8,128)S(1)}, f32[8,128]{1,0:T(8,128)S(1)}, u32[]{:S(2)}, u32[]{:S(2)}) %collective-permute-start.3) | collective-permute-done | bytes 4128 | tf_op jit(solution)/shard_map/ppermute | solution.py:296
  65.1 2.2 %collective-permute-done.2.refs_2_ = f32[8,128]{1,0:T(8,128)S(1)} collective-permute-done((f32[8,128]{1,0:T(8,128)S(1)}, f32[8,128]{1,0:T(8,128)S(1)}, u32[]{:S(2)}, u32[]{:S(2)}) %collective-permute-start.2) | collective-permute-done | bytes 4128 | tf_op jit(solution)/shard_map/ppermute | solution.py:296
  67.3 0.0 copy-done
  67.3 1.2 %shard_map.88 = bf16[128,2048]{1,0:T(8,128)(2,1)} custom-call(bf16[8,128,256]{2,1,0:T(8,128)(2,1)S(1)} %all_to_all.16.y_ref.refs_0_, f32[8,128]{1,0:T(8,128)S(1)} %shard_map.87.refs_1_, f32[8,128]{1,0:T(8,128)S(1)} %collective-permute-done.2.refs_2_, f32[8,128]{1,0:T(8,128)S(1)} %collective-permute-done.3.refs_3_, ...), custom_call_target="tpu_custom_call" | custom-call | tf_op jit(solution)/shard_map/pallas_call | solution.py:241
Async XLA Ops:
  2.5 21.9 %copy-start.1 = (f32[32]{0:T(128)S(1)}, f32[32]{0:T(128)}, u32[]{:S(2)}) copy-start(f32[32]{0:T(128)} %rate_ref.1) | copy-start | bytes 388
  24.4 18.7 %copy-start.2 = (f32[32]{0:T(128)S(1)}, f32[32]{0:T(128)}, u32[]{:S(2)}) copy-start(f32[32]{0:T(128)} %weight_ref.1) | copy-start | bytes 388
  27.8 8.7 %collective-permute-start = (bf16[2,264,256]{2,1,0:T(8,128)(2,1)}, bf16[2,264,256]{2,1,0:T(8,128)(2,1)S(1)}, u32[]{:S(2)}, u32[]{:S(2)}) collective-permute-start(bf16[2,264,256]{2,1,0:T(8,128)(2,1)} %get-tuple-element.23), channel_id=1, source_target_pairs={{0,16},{16,32},{32,48},{1,17},{17,33},{33,49},{2,18},{18,34},{34,5... | collective-permute-start | bytes 811016 | tf_op jit(solution)/shard_map/ppermute | solution.py:276
  31.4 11.7 %all-to-all-start.1 = ((bf16[8,128,256]{2,1,0:T(8,128)(2,1)}), bf16[8,128,256]{2,1,0:T(8,128)(2,1)S(1)}, u32[]{:S(2)}, u32[]{:S(2)}) async-start(bf16[8,128,256]{2,1,0:T(8,128)(2,1)} %get-tuple-element.18), calls=%async_computation.1 | async-start | bytes 1048576 | tf_op jit(solution)/shard_map/all_to_all | solution.py:277
  37.3 8.6 %collective-permute-start.1 = (bf16[2,256,256]{2,1,0:T(8,128)(2,1)}, bf16[2,256,256]{2,1,0:T(8,128)(2,1)}, u32[]{:S(2)}, u32[]{:S(2)}) collective-permute-start(bf16[2,256,256]{2,1,0:T(8,128)(2,1)} %shard_map.85), channel_id=1, source_target_pairs={{16,32},{32,48},{17,33},{33,49},{18,34},{34,50},{19,35},{35,51},{2... | collective-permute-start | bytes 786440 | tf_op jit(solution)/shard_map/ppermute | solution.py:279
  47.3 20.0 %copy-start = (f32[2048]{0:T(1024)S(1)}, f32[2048]{0:T(1024)}, u32[]{:S(2)}) copy-start(f32[2048]{0:T(1024)} %param.13) | copy-start | bytes 24580
  59.9 3.0 %collective-permute-start.4 = (f32[8,128]{1,0:T(8,128)S(1)}, f32[8,128]{1,0:T(8,128)S(1)}, u32[]{:S(2)}, u32[]{:S(2)}) collective-permute-start(f32[8,128]{1,0:T(8,128)S(1)} %shard_map.87.refs_1_), channel_id=1, source_target_pairs={{0,3},{1,0},{2,1},{3,2},{4,7},{5,4},{6,5},{7,6},{8,11},{9,8},{10,9... | collective-permute-start | bytes 12296 | tf_op jit(solution)/shard_map/ppermute | solution.py:296
  59.9 5.2 %collective-permute-start.3 = (f32[8,128]{1,0:T(8,128)S(1)}, f32[8,128]{1,0:T(8,128)S(1)}, u32[]{:S(2)}, u32[]{:S(2)}) collective-permute-start(f32[8,128]{1,0:T(8,128)S(1)} %shard_map.87.refs_1_), channel_id=1, source_target_pairs={{0,2},{1,3},{2,0},{3,1},{4,6},{5,7},{6,4},{7,5},{8,10},{9,11},{10,... | collective-permute-start | bytes 12296 | tf_op jit(solution)/shard_map/ppermute | solution.py:296
  62.7 4.5 %collective-permute-start.2 = (f32[8,128]{1,0:T(8,128)S(1)}, f32[8,128]{1,0:T(8,128)S(1)}, u32[]{:S(2)}, u32[]{:S(2)}) collective-permute-start(f32[8,128]{1,0:T(8,128)S(1)} %shard_map.87.refs_1_), channel_id=1, source_target_pairs={{0,1},{1,2},{2,3},{3,0},{4,5},{5,6},{6,7},{7,4},{8,9},{9,10},{10,1... | collective-permute-start | bytes 12296 | tf_op jit(solution)/shard_map/ppermute | solution.py:296

commit v2 on v1

--- a/solution.py
+++ b/solution.py
@@ -30,7 +30,7 @@
 
 
 def pack_kernel(
-    tok_ref, bc_ref, dt_ref, route_ref, seg_ref, out_ref, c_ref, bc_buf, dt_buf, route_buf, seg_buf, sems
+    tok_ref, bc_ref, dt_ref, route_ref, seg_ref, out_ref, c_ref, bc_buf, dt_buf, route_buf, seg_buf, wide_ref, sems
 ):
     small = ((route_ref, route_buf), (dt_ref, dt_buf), (seg_ref, seg_buf), (bc_ref, bc_buf))
     copies = [pltpu.make_async_copy(a, b, sems.at[n]) for n, (a, b) in enumerate(small)]
@@ -64,12 +64,14 @@
             aux = jnp.where(row == h, dt_rows[o * 4 + h : o * 4 + h + 1], aux)
         out_ref[o, TOK : TOK + AUX, :] = jnp.concatenate([aux.astype(BF16)] * 4, axis=1)
     copies[3].wait()
-    for g in range(2):
-        b = bc_buf[:, 0, g * WIDE : (g + 1) * WIDE]
-        c = bc_buf[:, 1, g * WIDE : (g + 1) * WIDE]
+    wide_ref[...] = bc_buf[...].astype(F32)
+    for tile in range(4):
+        g, half = tile // 2, tile % 2
+        b = wide_ref[pl.ds(2 * tile, TOK, stride=8), :].astype(BF16)
+        c = wide_ref[pl.ds(2 * tile + 1, TOK, stride=8), :].astype(BF16)
         for o in range(g * 4, g * 4 + 4):
-            out_ref[o, :TOK, WIDE : 2 * WIDE] = b
-            c_ref[o] = c
+            out_ref[o, :TOK, WIDE + half * TOK : WIDE + (half + 1) * TOK] = b
+            c_ref[o, :, half * TOK : (half + 1) * TOK] = c
     for copy in copies[4:]:
         copy.wait()
 
@@ -112,44 +114,66 @@
     return [key_of(*p) for p in rows], [key_of(*p) for p in cols], first, last
 
 
-def state_kernel(rate_ref, r_ref, e_ref, f_ref, xs_ref, own_ref, m_ref, dt_ref, bm_ref):
+def three(x, lane):
+    top = x.astype(BF16).astype(F32)
+    rest = x - top
+    mid = rest.astype(BF16).astype(F32)
+    return jnp.where(lane < 32, top, jnp.where(lane < 64, mid, jnp.where(lane < 96, rest - mid, 0.0))).astype(BF16)
+
+
+def state_kernel(rate_ref, r_ref, e_ref, f_ref, xs_ref, own_ref, bt_ref):
     rate = rate_lanes(rate_ref)
+    lane = iota((1, TOK), 1)
+    key = lane % 32 // 4
+    row, col = iota((AUX, TOK), 0), iota((AUX, TOK), 1)
+    code_of = jnp.where(row == 5, 1.0, jnp.where(row == 4, 2048.0, 0.0)).astype(BF16)
+    dt_of = ones_where(row == col % 4, BF16)
     spread = ones_where(iota((AUX, WIDE), 1) // 64 == iota((AUX, WIDE), 0), BF16)
-    key_rows, key_cols, first, last = keys_of(r_ref)
-    causal = iota((TOK, TOK), 0) >= iota((TOK, TOK), 1)
-    for i in range(PEERS):
-        src = (i % 2) * 4 + i // 2
-        dt_ref[i * TOK : (i + 1) * TOK, :] = dot(r_ref[src, TOK : TOK + AUX, 0:TOK], spread, ((0,), (0,))).astype(BF16)
-        for jj in range(i + 1 + (i + 1) % 2):
-            if jj > i:
-                m = jnp.zeros((TOK, TOK), BF16)
-            else:
-                same = key_cols[i] == key_rows[jj]
-                m = ones_where(same & causal if i == jj else same, BF16)
-            m_ref[i * TOK : (i + 1) * TOK, jj * TOK : (jj + 1) * TOK] = m
+    columns = jnp.concatenate([code_of, dt_of, spread], axis=1)
+    expand = ones_where(iota((TOK, WIDE), 0) % 4 == iota((TOK, WIDE), 1) // 64, BF16)
+    lower = ones_where(iota((256, 256), 0) >= iota((256, 256), 1), BF16)
+    auxs = [r_ref[q % 2 * 4 + q // 2, TOK : TOK + AUX, 0:TOK] for q in range(PEERS)]
+    auxf = [a.astype(F32) for a in auxs]
+    starts = [[sum(auxf[2 * y + d][6:7, k : k + 1] for y in range(4)) for k in range(3)] for d in range(2)]
+    first = [sum(ones_where(starts[d][k] <= 0.0) for k in range(3)) for d in range(2)]
+    last = [sum(ones_where(starts[d][k] <= SPAN - 1.0) for k in range(3)) for d in range(2)]
+    low, high = jnp.zeros((1, TOK), F32), jnp.zeros((1, TOK), F32)
+    final = []
+    for d in range(2):
+        edges = [jnp.zeros((1, 1), F32)] + starts[d] + [jnp.full((1, 1), float(SPAN), F32)]
+        at = edges[0]
+        for n in range(4):
+            low = jnp.where(key == 4 * d + n, edges[n] + 2048.0 * d, low)
+            high = jnp.where(key == 4 * d + n, edges[n + 1] + 2048.0 * d, high)
+            at = jnp.where(last[d] == n, edges[n], at)
+        final.append(at + 2048.0 * d)
+    for q in range(PEERS):
+        code = auxf[q][4:5] * 2048.0 + auxf[q][5:6] + (q // 2) * 256.0
+        bt = jnp.transpose(r_ref[q % 2 * 4 + q // 2, :TOK, WIDE : 2 * WIDE])
         for d in range(2):
-            lm = ones_where(key_cols[i] == last[d] + 4.0 * d, BF16)
-            for half in range(2):
-                bm_ref[d, i * TOK : (i + 1) * TOK, half * TOK : (half + 1) * TOK] = (
-                    r_ref[src, :TOK, WIDE + half * TOK : WIDE + (half + 1) * TOK] * lm
-                )
+            ends = jnp.broadcast_to(ones_where((code >= final[d]) & (code < 2048.0 * (d + 1))), (16, TOK)).astype(BF16)
+            bt_ref[d, :, q * TOK : (q + 1) * TOK] = bt * ends[0:1]
+    total = jnp.zeros((1, TOK), F32)
     for b in range(4):
-        sl = slice(b * 256, (b + 1) * 256)
-        total = dot(m_ref[sl, : (b + 1) * 256], dt_ref[: (b + 1) * 256, :], ((1,), (0,)))
-        f_ref[sl, :] = jnp.exp(-rate * total)
-        grow = jnp.exp(rate * total) * dt_ref[sl, :].astype(F32)
+        parts = [dot(auxs[2 * b + s], columns, ((0,), (0,))) for s in range(2)]
+        part = jnp.concatenate(parts, axis=0)
+        code = part[:, 0:TOK] + b * 256.0
+        mine = (code >= low) & (code < high)
+        z = jnp.where(mine, part[:, TOK : 2 * TOK], 0.0).astype(BF16)
+        sums = dot(lower, z, ((1,), (0,))) + total
+        total = sums[255:256]
+        d_wide = dot(three(jnp.where(mine, sums, 0.0), lane), expand, ((1,), (0,)))
+        f_ref[b * 256 : (b + 1) * 256, :] = jnp.exp(-rate * d_wide)
+        grow = jnp.exp(rate * d_wide) * part[:, 2 * TOK :]
         for s in range(2):
             x = r_ref[s * 4 + b, :TOK, 0:WIDE].astype(F32)
             at = b * 256 + s * TOK
             xs_ref[at : at + TOK, :] = (x * grow[s * TOK : (s + 1) * TOK]).astype(BF16)
     row8 = iota((AUX, WIDE), 0)
     for d in range(2):
-        total = jnp.zeros((AUX, WIDE), F32)
-        for q in range(PEERS):
-            lm = jnp.broadcast_to(ones_where(key_rows[q] == last[d] + 4.0 * d), (AUX, TOK)).astype(BF16)
-            total = total + dot(lm, dt_ref[q * TOK : (q + 1) * TOK, :], ((1,), (0,)))
-        through = jnp.exp(-rate * total)
-        e = dot(bm_ref[d], xs_ref[...], ((0,), (0,))) * through[0:1]
+        tail = jnp.broadcast_to(jnp.where(key == last[d].astype(jnp.int32) + 4 * d, total, 0.0), (AUX, TOK))
+        through = jnp.exp(-rate * dot(three(tail, lane), expand, ((1,), (0,))))
+        e = dot(bt_ref[d], xs_ref[...], ((1,), (0,))) * through[0:1]
         e_ref[d, 0:WIDE, :] = e.astype(BF16)
         e_ref[d, WIDE : WIDE + AUX, :] = jnp.broadcast_to(last[d], (AUX, WIDE)).astype(BF16)
         own_ref[d] = jnp.where(row8 == 0, jnp.where(first[d] == last[d], through, 0.0), first[d])
@@ -213,8 +237,12 @@
     s_ref[...] = dot(jnp.ones((AUX, WIDE), F32), acc, ((1,), (1,)), HIGH)
 
 
-def scale_kernel(y_ref, s0_ref, s1_ref, s2_ref, s3_ref, gain_ref, out_ref, *, features):
-    total = (s0_ref[...] + s1_ref[...]) + (s2_ref[...] + s3_ref[...])
+def add_kernel(a_ref, b_ref, out_ref):
+    out_ref[...] = a_ref[...] + b_ref[...]
+
+
+def scale_kernel(y_ref, s0_ref, s1_ref, gain_ref, out_ref, *, features):
+    total = s0_ref[...] + s1_ref[...]
     pick = ones_where(iota((AUX, TOK), 0) == 0)
     col = dot(total, pick, ((0,), (0,)), HIGH)
     scale = lax.rsqrt(col / features + EPSILON)
@@ -250,16 +278,18 @@
 
 def whole(tokens, bc_proj, step_sizes, decay_rates, direct_weight, norm_gain, routes, segments):
     V = pltpu.VMEM
+    pairs = bc_proj.reshape(TOK, 2, 4, TOK).transpose(0, 2, 1, 3).reshape(8 * TOK, TOK)
     send, send_c = call(
         pack_kernel,
         [HB] * 5,
         [V((PEERS, TOK + AUX, 2 * WIDE), BF16), pltpu.HBM((PEERS, TOK, WIDE), BF16)],
-        far(tokens[0]), far(bc_proj[0]), far(step_sizes[0]), far(routes.reshape(1, 16)), far(segments),
+        far(tokens[0]), far(pairs), far(step_sizes[0]), far(routes.reshape(1, 16)), far(segments),
         scratch=[
-            V((TOK, 2, 2 * WIDE), BF16),
+            V((8 * TOK, TOK), BF16),
             V((16, 256), BF16),
             V((1, 16), jnp.int32),
             V((1, 256), jnp.int32),
+            V((8 * TOK, TOK), F32),
             pltpu.SemaphoreType.DMA((4 + PEERS,)),
         ],
     )
@@ -269,12 +299,12 @@
         [SM, VM],
         [pltpu.HBM((2, WIDE + AUX, WIDE), BF16), V((SPAN, WIDE), F32), V((SPAN, WIDE), BF16), V((2, AUX, WIDE), F32)],
         decay_rates, got,
-        scratch=[V((SPAN, SPAN), BF16), V((SPAN, WIDE), BF16), V((2, SPAN, WIDE), BF16)],
+        scratch=[V((2, WIDE, SPAN), BF16)],
     )
     f, xs, own = kept(f), kept(xs), kept(own)
     e, send_c = lax.optimization_barrier((e, send_c))
     e1 = kept(lax.ppermute(e, "z", [(i, i + 1) for i in range(3)]))
-    got_c = kept(lax.all_to_all(send_c, ("dp", "y"), split_axis=0, concat_axis=0, tiled=True))
+    got_c = far(lax.all_to_all(send_c, ("dp", "y"), split_axis=0, concat_axis=0, tiled=True))
     (older,) = call(pass_kernel, [VM, VM], [pltpu.HBM((2, WIDE, WIDE), BF16)], e1, own)
     e2 = kept(lax.ppermute(older, "z", [(i, i + 1) for i in range(1, 3)]))
     base, cm = call(
@@ -293,13 +323,15 @@
     )
     back = kept(lax.all_to_all(out, ("dp", "y"), split_axis=0, concat_axis=0, tiled=True))
     (s0,) = call(square_kernel, [VM], [V((AUX, TOK), F32)], back)
-    others = [kept(lax.ppermute(s0, "tensor", [(i, (i + k) % 4) for i in range(4)])) for k in (1, 2, 3)]
+    t0 = lax.ppermute(s0, "tensor", [(i, i ^ 1) for i in range(4)])
+    (s0,) = call(add_kernel, [VM] * 2, [V((AUX, TOK), F32)], kept(s0), kept(t0))
+    others = [kept(lax.ppermute(s0, "tensor", [(i, i ^ 2) for i in range(4)]))]
 
     def scale(*refs):
         scale_kernel(*refs, features=128 * 64)
 
     out_shape = [jax.ShapeDtypeStruct((TOK, PEERS * WIDE), BF16)]
-    (mixed,) = call(scale, [VM] * 6, out_shape, back, kept(s0), *others, norm_gain[None])
+    (mixed,) = call(scale, [VM] * 4, out_shape, back, kept(s0), *others, norm_gain[None])
     return mixed[None]
 
 

time: 68.8 us -> 66.7 us (0.969)
  waiting for transfers between devices: 9 us -> 7.6 us
  Pallas kernels: 11.6 us -> 10.4 us
    pallas_call x7 -> x8, Pallas kernels: 11.6 us -> 10.4 us  [call(): pl.pallas_call(kernel, in_specs=specs, out_specs=[VM] * len(outs), out_sh...]
    ppermute x3 -> x2, waiting for transfers between devices: 4.33 us -> 3.58 us  [the longest x1 2.39 us: whole(): others = [kept(lax.ppermute(s0, 'tensor', [(i, i ^ 2) for i in range(4)]))]]
    ppermute x1, waiting for transfers between devices: 0.74 us -> 0.01 us  [whole(): e2 = kept(lax.ppermute(older, 'z', [(i, i + 1) for i in range(1, 3)]))]
    all_to_all x1, waiting for transfers between devices: 2.27 us -> 3 us  [whole(): lax.all_to_all(send_c, ('dp', 'y'), split_axis=0, concat_axis=0, tiled=True)]
    ppermute x3 -> x2, starting transfers between devices: 2.99 us -> 2.73 us  [the longest x1 2.73 us: whole(): others = [kept(lax.ppermute(s0, 'tensor', [(i, i ^ 2) for i in range(4)]))]]
  transfers between devices with their start and end apart: 6 -> 5, of which waited for: 5 -> 4; matrix products, arithmetic and copies ran while one was open for 0% -> 0% of each run, Pallas kernels for 4% -> 5%
where the time goes in v2:
time: 66.7 us; the launch traced here: 66.3 us
  blocking collectives  34.3 us (51%)
  starting transfers between devices  13.9 us (21%)
  Pallas kernels  10.4 us (16%)
  waiting for transfers between devices  7.6 us (11%)
    all_to_all x1, blocking collectives, whole(): lax.all_to_all(send, ('dp', 'y'), split_axis=0, concat_axis=0, tiled=True)  21.9 us
    all_to_all x1, blocking collectives, whole(): lax.all_to_all(out, ('dp', 'y'), split_axis=0, concat_axis=0, tiled=True)  12.4 us
    pallas_call x8, Pallas kernels, call(): pl.pallas_call(kernel, in_specs=specs, out_specs=[VM] * len(outs), out_sh...  10.4 us
    all_to_all x1, starting transfers between devices, whole(): lax.all_to_all(send_c, ('dp', 'y'), split_axis=0, concat_axis=0, tiled=True)  4.16 us
    ppermute x1, starting transfers between devices, whole(): e1 = kept(lax.ppermute(e, 'z', [(i, i + 1) for i in range(3)]))  3.52 us
    ppermute x1, starting transfers between devices, whole(): e2 = kept(lax.ppermute(older, 'z', [(i, i + 1) for i in range(1, 3)]))  3.51 us
    all_to_all x1, waiting for transfers between devices, whole(): lax.all_to_all(send_c, ('dp', 'y'), split_axis=0, concat_axis=0, tiled=True)  3 us
    ppermute x1, starting transfers between devices, whole(): others = [kept(lax.ppermute(s0, 'tensor', [(i, i ^ 2) for i in range(4)]))]  2.73 us
  transfers between devices with their start and end apart: 5, of which 4 were waited for; matrix products, arithmetic and copies ran while one was open for 0% of the time, Pallas kernels for 5%

profile of v2, /device:TPU:64, one launch (start us, length us, event | category | flops | bytes accessed | tf_op | source)
XLA Modules:
  0.0 66.3 jit_solution(2902528638290807394)
XLA Ops:
  0.0 2.2 %shard_map.82 = (bf16[8,136,512]{2,1,0:T(8,128)(2,1)S(1)}, bf16[8,128,256]{2,1,0:T(8,128)(2,1)}) custom-call(bf16[128,2048]{1,0:T(8,128)(2,1)} %bitcast.11, bf16[1024,128]{1,0:T(8,128)(2,1)} %bitcast.12, bf16[16,256]{1,0:T(8,128)(2,1)} %bitcast.13, s32[1,16]{1,0:T(1,128)} %bitcast.14, s32[1,256]{1,0:T(1,128)} %seg_ref.1), custom_call_target="tpu_custom_call" | custom-call | tf_op jit(solution)/shard_map/pallas_call | solution.py:269
  2.2 0.0 copy-start.1
  2.2 21.9 %all_to_all.15.r_ref = bf16[8,136,512]{2,1,0:T(8,128)(2,1)S(1)} all-to-all(bf16[8,136,512]{2,1,0:T(8,128)(2,1)S(1)} %get-tuple-element.15), channel_id=1, replica_groups=mesh['dp'=2,'z'=4,'y'=4,'tensor'=4] {'dp','y'}, dimensions={0} | all-to-all | bytes 2228224 | tf_op jit(solution)/shard_map/all_to_all | solution.py:296
  24.1 0.0 copy-done.1
  24.1 0.0 copy-start.2
  24.1 3.1 %shard_map.83 = (bf16[2,264,256]{2,1,0:T(8,128)(2,1)}, f32[1024,256]{1,0:T(8,128)S(1)}, bf16[1024,256]{1,0:T(8,128)(2,1)S(1)}, f32[2,8,256]{2,1,0:T(8,128)S(1)}) custom-call(f32[32]{0:T(128)S(1)} %copy-done.1, bf16[8,136,512]{2,1,0:T(8,128)(2,1)S(1)} %all_to_all.15.r_ref), custom_call_target="tpu_custom_call" | custom-call | tf_op jit(solution)/shard_map/pallas_call | solution.py:269
  27.2 3.5 %collective-permute-start = (bf16[2,264,256]{2,1,0:T(8,128)(2,1)}, bf16[2,264,256]{2,1,0:T(8,128)(2,1)S(1)}, u32[]{:S(2)}, u32[]{:S(2)}) collective-permute-start(bf16[2,264,256]{2,1,0:T(8,128)(2,1)} %get-tuple-element.23), channel_id=1, source_target_pairs={{0,16},{16,32},{32,48},{1,17},{17,33},{33,49},{2,18},{18,34},{34,5... | collective-permute-start | bytes 811016 | tf_op jit(solution)/shard_map/ppermute | solution.py:306
  30.7 4.2 %all-to-all-start.1 = ((bf16[8,128,256]{2,1,0:T(8,128)(2,1)}), bf16[8,128,256]{2,1,0:T(8,128)(2,1)}, u32[]{:S(2)}, u32[]{:S(2)}) async-start(bf16[8,128,256]{2,1,0:T(8,128)(2,1)} %get-tuple-element.18), calls=%async_computation.1 | async-start | bytes 1048576 | tf_op jit(solution)/shard_map/all_to_all | solution.py:307
  34.9 1.0 %collective-permute-done.e_ref.e1_ref = bf16[2,264,256]{2,1,0:T(8,128)(2,1)S(1)} collective-permute-done((bf16[2,264,256]{2,1,0:T(8,128)(2,1)}, bf16[2,264,256]{2,1,0:T(8,128)(2,1)S(1)}, u32[]{:S(2)}, u32[]{:S(2)}) %collective-permute-start) | collective-permute-done | bytes 270368 | tf_op jit(solution)/shard_map/ppermute | solution.py:306
  35.9 0.7 %shard_map.85 = bf16[2,256,256]{2,1,0:T(8,128)(2,1)} custom-call(bf16[2,264,256]{2,1,0:T(8,128)(2,1)S(1)} %collective-permute-done.e_ref.e1_ref, f32[2,8,256]{2,1,0:T(8,128)S(1)} %get-tuple-element.24.own_ref), custom_call_target="tpu_custom_call" | custom-call | tf_op jit(solution)/shard_map/pallas_call | solution.py:269
  36.6 3.5 %collective-permute-start.1 = (bf16[2,256,256]{2,1,0:T(8,128)(2,1)}, bf16[2,256,256]{2,1,0:T(8,128)(2,1)S(1)}, u32[]{:S(2)}, u32[]{:S(2)}) collective-permute-start(bf16[2,256,256]{2,1,0:T(8,128)(2,1)} %shard_map.85), channel_id=1, source_target_pairs={{16,32},{32,48},{17,33},{33,49},{18,34},{34,50},{19,35},{35,51},{2... | collective-permute-start | bytes 786440 | tf_op jit(solution)/shard_map/ppermute | solution.py:309
  40.1 3.0 %all-to-all-done.1.got_ref = bf16[8,128,256]{2,1,0:T(8,128)(2,1)} async-done(((bf16[8,128,256]{2,1,0:T(8,128)(2,1)}), bf16[8,128,256]{2,1,0:T(8,128)(2,1)}, u32[]{:S(2)}, u32[]{:S(2)}) %all-to-all-start.1) | async-done | bytes 524320 | tf_op jit(solution)/shard_map/all_to_all | solution.py:307
  43.1 0.0 copy-done.2
  43.1 2.5 %shard_map.84 = (f32[1024,256]{1,0:T(8,128)S(1)}, bf16[1024,512]{1,0:T(8,128)(2,1)S(1)}) custom-call(f32[32]{0:T(128)S(1)} %copy-done.2, bf16[8,136,512]{2,1,0:T(8,128)(2,1)S(1)} %all_to_all.15.r_ref, bf16[8,128,256]{2,1,0:T(8,128)(2,1)} %all-to-all-done.1.got_ref, f32[1024,256]{1,0:T(8,128)S(1)} %get-tuple-element.19.f_ref, ...), custom_call_target="tpu_custom_call" | custom-call | tf_op jit(solution)/shard_map/pallas_call | solution.py:269
  45.7 0.0 collective-permute-done.1.e2_ref
  45.7 0.5 shard_map.86
  46.2 0.0 copy-start
  46.2 12.4 %all_to_all.16.y_ref.refs_0_ = bf16[8,128,256]{2,1,0:T(8,128)(2,1)S(1)} all-to-all(bf16[8,128,256]{2,1,0:T(8,128)(2,1)S(1)} %shard_map.86), channel_id=1, replica_groups=mesh['dp'=2,'z'=4,'y'=4,'tensor'=4] {'dp','y'}, dimensions={0} | all-to-all | bytes 1048576 | tf_op jit(solution)/shard_map/all_to_all | solution.py:324
  58.6 0.3 shard_map.87.a_ref
  58.8 0.0 collective-permute-start.2
  58.8 1.2 %collective-permute-done.2.b_ref = f32[8,128]{1,0:T(8,128)S(1)} collective-permute-done((f32[8,128]{1,0:T(8,128)S(1)}, f32[8,128]{1,0:T(8,128)S(1)}, u32[]{:S(2)}, u32[]{:S(2)}) %collective-permute-start.2) | collective-permute-done | bytes 4128 | tf_op jit(solution)/shard_map/ppermute | solution.py:326
  60.0 2.7 %collective-permute-start.3 = (f32[8,128]{1,0:T(8,128)S(1)}, f32[8,128]{1,0:T(8,128)S(1)}, u32[]{:S(2)}, u32[]{:S(2)}) collective-permute-start(f32[8,128]{1,0:T(8,128)S(1)} %shard_map.88.refs_1_), channel_id=1, source_target_pairs={{0,2},{1,3},{2,0},{3,1},{4,6},{5,7},{6,4},{7,5},{8,10},{9,11},{10,... | collective-permute-start | bytes 12296 | tf_op jit(solution)/shard_map/ppermute | solution.py:328
  62.8 2.4 %collective-permute-done.3.refs_2_ = f32[8,128]{1,0:T(8,128)S(1)} collective-permute-done((f32[8,128]{1,0:T(8,128)S(1)}, f32[8,128]{1,0:T(8,128)S(1)}, u32[]{:S(2)}, u32[]{:S(2)}) %collective-permute-start.3) | collective-permute-done | bytes 4128 | tf_op jit(solution)/shard_map/ppermute | solution.py:328
  65.2 0.0 copy-done
  65.2 1.2 %shard_map.89 = bf16[128,2048]{1,0:T(8,128)(2,1)} custom-call(bf16[8,128,256]{2,1,0:T(8,128)(2,1)S(1)} %all_to_all.16.y_ref.refs_0_, f32[8,128]{1,0:T(8,128)S(1)} %shard_map.88.refs_1_, f32[8,128]{1,0:T(8,128)S(1)} %collective-permute-done.3.refs_2_, f32[1,2048]{1,0:T(1,128)S(1)} %bitcast.10), custom_call_target="tpu_custom_call" | custom-call | tf_op jit(solution)/shard_map/pallas_call | solution.py:269
  (1 shorter events, 0.0 us)
Async XLA Ops:
  2.2 21.9 %copy-start.1 = (f32[32]{0:T(128)S(1)}, f32[32]{0:T(128)}, u32[]{:S(2)}) copy-start(f32[32]{0:T(128)} %rate_ref.1) | copy-start | bytes 388
  24.1 19.1 %copy-start.2 = (f32[32]{0:T(128)S(1)}, f32[32]{0:T(128)}, u32[]{:S(2)}) copy-start(f32[32]{0:T(128)} %weight_ref.1) | copy-start | bytes 388
  27.2 8.7 %collective-permute-start = (bf16[2,264,256]{2,1,0:T(8,128)(2,1)}, bf16[2,264,256]{2,1,0:T(8,128)(2,1)S(1)}, u32[]{:S(2)}, u32[]{:S(2)}) collective-permute-start(bf16[2,264,256]{2,1,0:T(8,128)(2,1)} %get-tuple-element.23), channel_id=1, source_target_pairs={{0,16},{16,32},{32,48},{1,17},{17,33},{33,49},{2,18},{18,34},{34,5... | collective-permute-start | bytes 811016 | tf_op jit(solution)/shard_map/ppermute | solution.py:306
  30.7 12.4 %all-to-all-start.1 = ((bf16[8,128,256]{2,1,0:T(8,128)(2,1)}), bf16[8,128,256]{2,1,0:T(8,128)(2,1)}, u32[]{:S(2)}, u32[]{:S(2)}) async-start(bf16[8,128,256]{2,1,0:T(8,128)(2,1)} %get-tuple-element.18), calls=%async_computation.1 | async-start | bytes 1048576 | tf_op jit(solution)/shard_map/all_to_all | solution.py:307
  36.6 9.1 %collective-permute-start.1 = (bf16[2,256,256]{2,1,0:T(8,128)(2,1)}, bf16[2,256,256]{2,1,0:T(8,128)(2,1)S(1)}, u32[]{:S(2)}, u32[]{:S(2)}) collective-permute-start(bf16[2,256,256]{2,1,0:T(8,128)(2,1)} %shard_map.85), channel_id=1, source_target_pairs={{16,32},{32,48},{17,33},{33,49},{18,34},{34,50},{19,35},{35,51},{2... | collective-permute-start | bytes 786440 | tf_op jit(solution)/shard_map/ppermute | solution.py:309
  46.2 19.0 %copy-start = (f32[2048]{0:T(1024)S(1)}, f32[2048]{0:T(1024)}, u32[]{:S(2)}) copy-start(f32[2048]{0:T(1024)} %param.13) | copy-start | bytes 24580
  58.8 1.2 %collective-permute-start.2 = (f32[8,128]{1,0:T(8,128)S(1)}, f32[8,128]{1,0:T(8,128)S(1)}, u32[]{:S(2)}, u32[]{:S(2)}) collective-permute-start(f32[8,128]{1,0:T(8,128)S(1)} %shard_map.87.a_ref), channel_id=1, source_target_pairs={{0,1},{1,0},{2,3},{3,2},{4,5},{5,4},{6,7},{7,6},{8,9},{9,8},{10,11... | collective-permute-start | bytes 12296 | tf_op jit(solution)/shard_map/ppermute | solution.py:326
  60.0 5.1 %collective-permute-start.3 = (f32[8,128]{1,0:T(8,128)S(1)}, f32[8,128]{1,0:T(8,128)S(1)}, u32[]{:S(2)}, u32[]{:S(2)}) collective-permute-start(f32[8,128]{1,0:T(8,128)S(1)} %shard_map.88.refs_1_), channel_id=1, source_target_pairs={{0,2},{1,3},{2,0},{3,1},{4,6},{5,7},{6,4},{7,5},{8,10},{9,11},{10,... | collective-permute-start | bytes 12296 | tf_op jit(solution)/shard_map/ppermute | solution.py:328

commit v3 on v2

--- a/solution.py
+++ b/solution.py
@@ -30,16 +30,29 @@
 
 
 def pack_kernel(
-    tok_ref, bc_ref, dt_ref, route_ref, seg_ref, out_ref, c_ref, bc_buf, dt_buf, route_buf, seg_buf, wide_ref, sems
+    tok_ref, bc_ref, dt_ref, route_ref, seg_ref, out_ref, c_ref, bc_buf, dt_buf, route_buf, seg_buf, wide_ref, c_buf, sems
 ):
-    small = ((route_ref, route_buf), (dt_ref, dt_buf), (seg_ref, seg_buf), (bc_ref, bc_buf))
+    small = ((bc_ref, bc_buf), (route_ref, route_buf), (dt_ref, dt_buf), (seg_ref, seg_buf))
     copies = [pltpu.make_async_copy(a, b, sems.at[n]) for n, (a, b) in enumerate(small)]
     for o in range(PEERS):
         src = tok_ref.at[:, o * WIDE : (o + 1) * WIDE]
         copies.append(pltpu.make_async_copy(src, out_ref.at[o, 0:TOK, 0:WIDE], sems.at[4 + o]))
     for copy in copies:
         copy.start()
-    for copy in copies[:3]:
+    copies[0].wait()
+    wide_ref[...] = bc_buf[...].astype(F32)
+    for tile in range(4):
+        g, half = tile // 2, tile % 2
+        c_buf[g, :, half * TOK : (half + 1) * TOK] = wide_ref[pl.ds(2 * tile + 1, TOK, stride=8), :].astype(BF16)
+    for o in range(PEERS):
+        copies.append(pltpu.make_async_copy(c_buf.at[o // 4], c_ref.at[o], sems.at[4 + PEERS + o]))
+        copies[-1].start()
+    for tile in range(4):
+        g, half = tile // 2, tile % 2
+        b = wide_ref[pl.ds(2 * tile, TOK, stride=8), :].astype(BF16)
+        for o in range(g * 4, g * 4 + 4):
+            out_ref[o, :TOK, WIDE + half * TOK : WIDE + (half + 1) * TOK] = b
+    for copy in copies[1:4]:
         copy.wait()
     block_of = ones_where(iota((16, TOK), 1) // 8 == iota((16, TOK), 0), BF16)
     spread = dot(dt_buf[...], block_of, ((0,), (0,)))
@@ -63,15 +76,6 @@
         for h in range(4):
             aux = jnp.where(row == h, dt_rows[o * 4 + h : o * 4 + h + 1], aux)
         out_ref[o, TOK : TOK + AUX, :] = jnp.concatenate([aux.astype(BF16)] * 4, axis=1)
-    copies[3].wait()
-    wide_ref[...] = bc_buf[...].astype(F32)
-    for tile in range(4):
-        g, half = tile // 2, tile % 2
-        b = wide_ref[pl.ds(2 * tile, TOK, stride=8), :].astype(BF16)
-        c = wide_ref[pl.ds(2 * tile + 1, TOK, stride=8), :].astype(BF16)
-        for o in range(g * 4, g * 4 + 4):
-            out_ref[o, :TOK, WIDE + half * TOK : WIDE + (half + 1) * TOK] = b
-            c_ref[o, :, half * TOK : (half + 1) * TOK] = c
     for copy in copies[4:]:
         copy.wait()
 
@@ -163,7 +167,7 @@
         sums = dot(lower, z, ((1,), (0,))) + total
         total = sums[255:256]
         d_wide = dot(three(jnp.where(mine, sums, 0.0), lane), expand, ((1,), (0,)))
-        f_ref[b * 256 : (b + 1) * 256, :] = jnp.exp(-rate * d_wide)
+        f_ref[b * 256 : (b + 1) * 256, :] = jnp.exp(-rate * d_wide).astype(BF16)
         grow = jnp.exp(rate * d_wide) * part[:, 2 * TOK :]
         for s in range(2):
             x = r_ref[s * 4 + b, :TOK, 0:WIDE].astype(F32)
@@ -204,7 +208,7 @@
             same = keys == jnp.concatenate(key_rows[2 * j : 2 * j + 2], axis=1)
             w = jnp.where(same & causal if i == j else same, s, 0.0).astype(BF16)
             acc = acc + dot(w, xs_ref[sj, :], ((1,), (0,)))
-        acc = acc * f_ref[si, :]
+        acc = acc * f_ref[si, :].astype(F32)
         for s in range(2):
             x = r_ref[s * 4 + i, :TOK, 0:WIDE].astype(F32)
             at = i * 256 + s * TOK
@@ -225,7 +229,7 @@
         h_ref[d * WIDE : (d + 1) * WIDE, :] = jnp.where(joined, h, 0.0).astype(BF16)
     for q in range(PEERS):
         sl = slice(q * TOK, (q + 1) * TOK)
-        y = base_ref[sl, :] + f_ref[sl, :] * dot(cm_ref[sl, :], h_ref[...], ((1,), (0,)))
+        y = base_ref[sl, :] + f_ref[sl, :].astype(F32) * dot(cm_ref[sl, :], h_ref[...], ((1,), (0,)))
         y_ref[(q % 2) * 4 + q // 2] = y.astype(BF16)
 
 
@@ -265,11 +269,11 @@
     return pltpu.with_memory_space_constraint(x, pltpu.HBM)
 
 
-def call(kernel, specs, outs, *args, scratch=()):
+def call(kernel, specs, outs, *args, scratch=(), out_specs=None):
     return pl.pallas_call(
         kernel,
         in_specs=specs,
-        out_specs=[VM] * len(outs),
+        out_specs=out_specs or [VM] * len(outs),
         out_shape=outs,
         scratch_shapes=list(scratch),
         compiler_params=pltpu.CompilerParams(vmem_limit_bytes=14 << 20),
@@ -290,22 +294,24 @@
             V((1, 16), jnp.int32),
             V((1, 256), jnp.int32),
             V((8 * TOK, TOK), F32),
-            pltpu.SemaphoreType.DMA((4 + PEERS,)),
+            V((2, TOK, WIDE), BF16),
+            pltpu.SemaphoreType.DMA((4 + 2 * PEERS,)),
         ],
+        out_specs=[VM, HB],
     )
     got = kept(lax.all_to_all(send, ("dp", "y"), split_axis=0, concat_axis=0, tiled=True))
     e, f, xs, own = call(
         state_kernel,
         [SM, VM],
-        [pltpu.HBM((2, WIDE + AUX, WIDE), BF16), V((SPAN, WIDE), F32), V((SPAN, WIDE), BF16), V((2, AUX, WIDE), F32)],
+        [V((2, WIDE + AUX, WIDE), BF16), V((SPAN, WIDE), BF16), V((SPAN, WIDE), BF16), V((2, AUX, WIDE), F32)],
         decay_rates, got,
         scratch=[V((2, WIDE, SPAN), BF16)],
     )
     f, xs, own = kept(f), kept(xs), kept(own)
     e, send_c = lax.optimization_barrier((e, send_c))
     e1 = kept(lax.ppermute(e, "z", [(i, i + 1) for i in range(3)]))
-    got_c = far(lax.all_to_all(send_c, ("dp", "y"), split_axis=0, concat_axis=0, tiled=True))
-    (older,) = call(pass_kernel, [VM, VM], [pltpu.HBM((2, WIDE, WIDE), BF16)], e1, own)
+    got_c = kept(lax.all_to_all(send_c, ("dp", "y"), split_axis=0, concat_axis=0, tiled=True))
+    (older,) = call(pass_kernel, [VM, VM], [V((2, WIDE, WIDE), BF16)], e1, own)
     e2 = kept(lax.ppermute(older, "z", [(i, i + 1) for i in range(1, 3)]))
     base, cm = call(
         inside_kernel,

time: 66.7 us -> 64.2 us (0.963)
  Pallas kernels: 10.4 us -> 8.32 us
    pallas_call x8, Pallas kernels: 10.4 us -> 8.32 us  [call(): pl.pallas_call(kernel, in_specs=specs, out_specs=out_specs or [VM] * len(...]
  transfers between devices with their start and end apart: 5 -> 5, of which waited for: 4 -> 4; matrix products, arithmetic and copies ran while one was open for 0% -> 0% of each run, Pallas kernels for 5% -> 3%
where the time goes in v3:
time: 64.2 us; the launch traced here: 63.9 us
  blocking collectives  34 us (53%)
  starting transfers between devices  13.3 us (21%)
  Pallas kernels  8.32 us (13%)
  waiting for transfers between devices  8.19 us (13%)
    all_to_all x1, blocking collectives, whole(): lax.all_to_all(send, ('dp', 'y'), split_axis=0, concat_axis=0, tiled=True)  21.8 us
    all_to_all x1, blocking collectives, whole(): lax.all_to_all(out, ('dp', 'y'), split_axis=0, concat_axis=0, tiled=True)  12.1 us
    pallas_call x8, Pallas kernels, call(): pl.pallas_call(kernel, in_specs=specs, out_specs=out_specs or [VM] * len(...  8.32 us
    ppermute x1, starting transfers between devices, whole(): e1 = kept(lax.ppermute(e, 'z', [(i, i + 1) for i in range(3)]))  3.53 us
    ppermute x1, starting transfers between devices, whole(): e2 = kept(lax.ppermute(older, 'z', [(i, i + 1) for i in range(1, 3)]))  3.53 us
    all_to_all x1, starting transfers between devices, whole(): lax.all_to_all(send_c, ('dp', 'y'), split_axis=0, concat_axis=0, tiled=True)  3.51 us
    all_to_all x1, waiting for transfers between devices, whole(): lax.all_to_all(send_c, ('dp', 'y'), split_axis=0, concat_axis=0, tiled=True)  3.16 us
    ppermute x1, starting transfers between devices, whole(): others = [kept(lax.ppermute(s0, 'tensor', [(i, i ^ 2) for i in range(4)]))]  2.73 us
  transfers between devices with their start and end apart: 5, of which 4 were waited for; matrix products, arithmetic and copies ran while one was open for 0% of the time, Pallas kernels for 3%

profile of v3, /device:TPU:64, one launch (start us, length us, event | category | flops | bytes accessed | tf_op | source)
XLA Modules:
  0.0 63.9 jit_solution(13045620664564513235)
XLA Ops:
  0.0 2.0 %shard_map.82 = (bf16[8,136,512]{2,1,0:T(8,128)(2,1)S(1)}, bf16[8,128,256]{2,1,0:T(8,128)(2,1)}) custom-call(bf16[128,2048]{1,0:T(8,128)(2,1)} %bitcast.11, bf16[1024,128]{1,0:T(8,128)(2,1)} %bitcast.12, bf16[16,256]{1,0:T(8,128)(2,1)} %bitcast.13, s32[1,16]{1,0:T(1,128)} %bitcast.14, s32[1,256]{1,0:T(1,128)} %seg_ref.1), custom_call_target="tpu_custom_call" | custom-call | tf_op jit(solution)/shard_map/pallas_call | solution.py:273
  2.0 0.0 copy-start.1
  2.0 21.8 %all_to_all.15.r_ref = bf16[8,136,512]{2,1,0:T(8,128)(2,1)S(1)} all-to-all(bf16[8,136,512]{2,1,0:T(8,128)(2,1)S(1)} %get-tuple-element.15), channel_id=1, replica_groups=mesh['dp'=2,'z'=4,'y'=4,'tensor'=4] {'dp','y'}, dimensions={0} | all-to-all | bytes 2228224 | tf_op jit(solution)/shard_map/all_to_all | solution.py:302
  23.9 0.0 copy-done.1
  23.9 0.0 copy-start.2
  23.9 2.4 %shard_map.83 = (bf16[2,264,256]{2,1,0:T(8,128)(2,1)S(1)}, bf16[1024,256]{1,0:T(8,128)(2,1)S(1)}, bf16[1024,256]{1,0:T(8,128)(2,1)S(1)}, f32[2,8,256]{2,1,0:T(8,128)S(1)}) custom-call(f32[32]{0:T(128)S(1)} %copy-done.1, bf16[8,136,512]{2,1,0:T(8,128)(2,1)S(1)} %all_to_all.15.r_ref), custom_call_target="tpu_custom_call" | custom-call | tf_op jit(solution)/shard_map/pallas_call | solution.py:273
  26.2 3.5 %collective-permute-start = (bf16[2,264,256]{2,1,0:T(8,128)(2,1)S(1)}, bf16[2,264,256]{2,1,0:T(8,128)(2,1)S(1)}, u32[]{:S(2)}, u32[]{:S(2)}) collective-permute-start(bf16[2,264,256]{2,1,0:T(8,128)(2,1)S(1)} %get-tuple-element.23), channel_id=1, source_target_pairs={{0,16},{16,32},{32,48},{1,17},{17,33},{33,49},{2,18},{18,34},{34,5... | collective-permute-start | bytes 811016 | tf_op jit(solution)/shard_map/ppermute | solution.py:312
  29.8 3.5 %all-to-all-start.1 = ((bf16[8,128,256]{2,1,0:T(8,128)(2,1)}), bf16[8,128,256]{2,1,0:T(8,128)(2,1)S(1)}, u32[]{:S(2)}, u32[]{:S(2)}) async-start(bf16[8,128,256]{2,1,0:T(8,128)(2,1)} %get-tuple-element.18), calls=%async_computation.1 | async-start | bytes 1048576 | tf_op jit(solution)/shard_map/all_to_all | solution.py:313
  33.3 1.5 %collective-permute-done.e_ref.e1_ref = bf16[2,264,256]{2,1,0:T(8,128)(2,1)S(1)} collective-permute-done((bf16[2,264,256]{2,1,0:T(8,128)(2,1)S(1)}, bf16[2,264,256]{2,1,0:T(8,128)(2,1)S(1)}, u32[]{:S(2)}, u32[]{:S(2)}) %collective-permute-start) | collective-permute-done | bytes 270368 | tf_op jit(solution)/shard_map/ppermute | solution.py:312
  34.8 3.5 %collective-permute-start.1 = (bf16[2,256,256]{2,1,0:T(8,128)(2,1)S(1)}, bf16[2,256,256]{2,1,0:T(8,128)(2,1)S(1)}, u32[]{:S(2)}, u32[]{:S(2)}) collective-permute-start(bf16[2,256,256]{2,1,0:T(8,128)(2,1)S(1)} %shard_map.85), channel_id=1, source_target_pairs={{16,32},{32,48},{17,33},{33,49},{18,34},{34,50},{19,35},{35,51},{2... | collective-permute-start | bytes 786440 | tf_op jit(solution)/shard_map/ppermute | solution.py:315
  38.3 3.2 %all-to-all-done.1.got_ref = bf16[8,128,256]{2,1,0:T(8,128)(2,1)S(1)} async-done(((bf16[8,128,256]{2,1,0:T(8,128)(2,1)}), bf16[8,128,256]{2,1,0:T(8,128)(2,1)S(1)}, u32[]{:S(2)}, u32[]{:S(2)}) %all-to-all-start.1) | async-done | bytes 524320 | tf_op jit(solution)/shard_map/all_to_all | solution.py:313
  41.5 0.0 copy-done.2
  41.5 2.0 %shard_map.84 = (f32[1024,256]{1,0:T(8,128)S(1)}, bf16[1024,512]{1,0:T(8,128)(2,1)S(1)}) custom-call(f32[32]{0:T(128)S(1)} %copy-done.2, bf16[8,136,512]{2,1,0:T(8,128)(2,1)S(1)} %all_to_all.15.r_ref, bf16[8,128,256]{2,1,0:T(8,128)(2,1)S(1)} %all-to-all-done.1.got_ref, bf16[1024,256]{1,0:T(8,128)(2,1)S(1)} %get-tuple-element.19.f_ref, ...), custom_call_target="tpu_custom_call" | custom-call | tf_op jit(solution)/shard_map/pallas_call | solution.py:273
  43.5 0.0 collective-permute-done.1.e2_ref
  43.5 0.5 shard_map.86
  44.0 0.0 copy-start
  44.0 12.1 %all_to_all.16.y_ref.refs_0_ = bf16[8,128,256]{2,1,0:T(8,128)(2,1)S(1)} all-to-all(bf16[8,128,256]{2,1,0:T(8,128)(2,1)S(1)} %shard_map.86), channel_id=1, replica_groups=mesh['dp'=2,'z'=4,'y'=4,'tensor'=4] {'dp','y'}, dimensions={0} | all-to-all | bytes 1048576 | tf_op jit(solution)/shard_map/all_to_all | solution.py:330
  56.1 0.3 shard_map.87.a_ref
  56.4 0.0 collective-permute-start.2
  56.4 1.2 %collective-permute-done.2.b_ref = f32[8,128]{1,0:T(8,128)S(1)} collective-permute-done((f32[8,128]{1,0:T(8,128)S(1)}, f32[8,128]{1,0:T(8,128)S(1)}, u32[]{:S(2)}, u32[]{:S(2)}) %collective-permute-start.2) | collective-permute-done | bytes 4128 | tf_op jit(solution)/shard_map/ppermute | solution.py:332
  57.6 2.7 %collective-permute-start.3 = (f32[8,128]{1,0:T(8,128)S(1)}, f32[8,128]{1,0:T(8,128)S(1)}, u32[]{:S(2)}, u32[]{:S(2)}) collective-permute-start(f32[8,128]{1,0:T(8,128)S(1)} %shard_map.88.refs_1_), channel_id=1, source_target_pairs={{0,2},{1,3},{2,0},{3,1},{4,6},{5,7},{6,4},{7,5},{8,10},{9,11},{10,... | collective-permute-start | bytes 12296 | tf_op jit(solution)/shard_map/ppermute | solution.py:334
  60.3 2.4 %collective-permute-done.3.refs_2_ = f32[8,128]{1,0:T(8,128)S(1)} collective-permute-done((f32[8,128]{1,0:T(8,128)S(1)}, f32[8,128]{1,0:T(8,128)S(1)}, u32[]{:S(2)}, u32[]{:S(2)}) %collective-permute-start.3) | collective-permute-done | bytes 4128 | tf_op jit(solution)/shard_map/ppermute | solution.py:334
  62.7 0.0 copy-done
  62.7 1.2 %shard_map.89 = bf16[128,2048]{1,0:T(8,128)(2,1)} custom-call(bf16[8,128,256]{2,1,0:T(8,128)(2,1)S(1)} %all_to_all.16.y_ref.refs_0_, f32[8,128]{1,0:T(8,128)S(1)} %shard_map.88.refs_1_, f32[8,128]{1,0:T(8,128)S(1)} %collective-permute-done.3.refs_2_, f32[1,2048]{1,0:T(1,128)S(1)} %bitcast.10), custom_call_target="tpu_custom_call" | custom-call | tf_op jit(solution)/shard_map/pallas_call | solution.py:273
  (2 shorter events, 0.1 us)
Async XLA Ops:
  2.0 21.9 %copy-start.1 = (f32[32]{0:T(128)S(1)}, f32[32]{0:T(128)}, u32[]{:S(2)}) copy-start(f32[32]{0:T(128)} %rate_ref.1) | copy-start | bytes 388
  23.9 17.6 %copy-start.2 = (f32[32]{0:T(128)S(1)}, f32[32]{0:T(128)}, u32[]{:S(2)}) copy-start(f32[32]{0:T(128)} %weight_ref.1) | copy-start | bytes 388
  26.2 8.5 %collective-permute-start = (bf16[2,264,256]{2,1,0:T(8,128)(2,1)S(1)}, bf16[2,264,256]{2,1,0:T(8,128)(2,1)S(1)}, u32[]{:S(2)}, u32[]{:S(2)}) collective-permute-start(bf16[2,264,256]{2,1,0:T(8,128)(2,1)S(1)} %get-tuple-element.23), channel_id=1, source_target_pairs={{0,16},{16,32},{32,48},{1,17},{17,33},{33,49},{2,18},{18,34},{34,5... | collective-permute-start | bytes 811016 | tf_op jit(solution)/shard_map/ppermute | solution.py:312
  29.8 11.7 %all-to-all-start.1 = ((bf16[8,128,256]{2,1,0:T(8,128)(2,1)}), bf16[8,128,256]{2,1,0:T(8,128)(2,1)S(1)}, u32[]{:S(2)}, u32[]{:S(2)}) async-start(bf16[8,128,256]{2,1,0:T(8,128)(2,1)} %get-tuple-element.18), calls=%async_computation.1 | async-start | bytes 1048576 | tf_op jit(solution)/shard_map/all_to_all | solution.py:313
  34.8 8.7 %collective-permute-start.1 = (bf16[2,256,256]{2,1,0:T(8,128)(2,1)S(1)}, bf16[2,256,256]{2,1,0:T(8,128)(2,1)S(1)}, u32[]{:S(2)}, u32[]{:S(2)}) collective-permute-start(bf16[2,256,256]{2,1,0:T(8,128)(2,1)S(1)} %shard_map.85), channel_id=1, source_target_pairs={{16,32},{32,48},{17,33},{33,49},{18,34},{34,50},{19,35},{35,51},{2... | collective-permute-start | bytes 786440 | tf_op jit(solution)/shard_map/ppermute | solution.py:315
  44.0 18.7 %copy-start = (f32[2048]{0:T(1024)S(1)}, f32[2048]{0:T(1024)}, u32[]{:S(2)}) copy-start(f32[2048]{0:T(1024)} %param.13) | copy-start | bytes 24580
  56.4 1.2 %collective-permute-start.2 = (f32[8,128]{1,0:T(8,128)S(1)}, f32[8,128]{1,0:T(8,128)S(1)}, u32[]{:S(2)}, u32[]{:S(2)}) collective-permute-start(f32[8,128]{1,0:T(8,128)S(1)} %shard_map.87.a_ref), channel_id=1, source_target_pairs={{0,1},{1,0},{2,3},{3,2},{4,5},{5,4},{6,7},{7,6},{8,9},{9,8},{10,11... | collective-permute-start | bytes 12296 | tf_op jit(solution)/shard_map/ppermute | solution.py:332
  57.6 5.1 %collective-permute-start.3 = (f32[8,128]{1,0:T(8,128)S(1)}, f32[8,128]{1,0:T(8,128)S(1)}, u32[]{:S(2)}, u32[]{:S(2)}) collective-permute-start(f32[8,128]{1,0:T(8,128)S(1)} %shard_map.88.refs_1_), channel_id=1, source_target_pairs={{0,2},{1,3},{2,0},{3,1},{4,6},{5,7},{6,4},{7,5},{8,10},{9,11},{10,... | collective-permute-start | bytes 12296 | tf_op jit(solution)/shard_map/ppermute | solution.py:334

commit v4 on v3

--- a/solution.py
+++ b/solution.py
@@ -14,6 +14,7 @@
 PEERS = 8
 SPAN = TOK * PEERS
 WIDE = 256
+AT = 2 * TOK
 AUX = 8
 
 
@@ -51,7 +52,7 @@
         g, half = tile // 2, tile % 2
         b = wide_ref[pl.ds(2 * tile, TOK, stride=8), :].astype(BF16)
         for o in range(g * 4, g * 4 + 4):
-            out_ref[o, :TOK, WIDE + half * TOK : WIDE + (half + 1) * TOK] = b
+            out_ref[o, TOK:AT, half * TOK : (half + 1) * TOK] = b
     for copy in copies[1:4]:
         copy.wait()
     block_of = ones_where(iota((16, TOK), 1) // 8 == iota((16, TOK), 0), BF16)
@@ -75,7 +76,7 @@
         aux = jnp.where(row == 4, route_row[0:1], jnp.where(row == 5, place, starts))
         for h in range(4):
             aux = jnp.where(row == h, dt_rows[o * 4 + h : o * 4 + h + 1], aux)
-        out_ref[o, TOK : TOK + AUX, :] = jnp.concatenate([aux.astype(BF16)] * 4, axis=1)
+        out_ref[o, AT : AT + AUX, :] = jnp.concatenate([aux.astype(BF16)] * 2, axis=1)
     for copy in copies[4:]:
         copy.wait()
 
@@ -90,32 +91,19 @@
 
 
 def keys_of(r_ref):
-    pick_route = ones_where(iota((AUX, TOK), 0) == 4, BF16)
-    pick_place = ones_where(iota((AUX, TOK), 0) == 5, BF16)
-    starts = [[None] * 3, [None] * 3]
+    auxf = [r_ref[q % 2 * 4 + q // 2, AT : AT + AUX, 0:TOK].astype(F32) for q in range(PEERS)]
+    starts = [[sum(auxf[2 * y + d][6:7, k : k + 1] for y in range(4)) for k in range(3)] for d in range(2)]
+    first = [sum(ones_where(starts[d][k] <= 0.0) for k in range(3)) for d in range(2)]
+    pick = ones_where(iota((AUX, TOK), 0) == 0, BF16)
     rows, cols = [], []
     for q in range(PEERS):
-        y, j = q // 2, q % 2
-        aux = r_ref[j * 4 + y, TOK : TOK + AUX, 0:TOK]
-        auxf = aux.astype(F32)
-        rows.append((auxf[4:5], auxf[5:6] + y * 256.0))
-        cols.append((dot(aux, pick_route, ((0,), (0,))), dot(aux, pick_place, ((0,), (0,))) + y * 256.0))
-        for k in range(3):
-            n = auxf[6:7, k : k + 1]
-            starts[j][k] = n if starts[j][k] is None else starts[j][k] + n
-
-    def key_of(route, place):
-        second = route > 0.5
+        route, place = auxf[q][4:5], auxf[q][5:6] + (q // 2) * 256.0
         doc = 4.0 * route
         for k in range(3):
-            doc = doc + ones_where(place >= jnp.where(second, starts[1][k], starts[0][k]))
-        return doc
-
-    first, last = [], []
-    for d in range(2):
-        first.append(sum(ones_where(starts[d][k] <= 0.0) for k in range(3)))
-        last.append(sum(ones_where(starts[d][k] <= SPAN - 1.0) for k in range(3)))
-    return [key_of(*p) for p in rows], [key_of(*p) for p in cols], first, last
+            doc = doc + ones_where(place >= jnp.where(route > 0.5, starts[1][k], starts[0][k]))
+        rows.append(doc)
+        cols.append(dot(jnp.broadcast_to(doc, (AUX, TOK)).astype(BF16), pick, ((0,), (0,))))
+    return rows, cols, first
 
 
 def three(x, lane):
@@ -136,7 +124,7 @@
     columns = jnp.concatenate([code_of, dt_of, spread], axis=1)
     expand = ones_where(iota((TOK, WIDE), 0) % 4 == iota((TOK, WIDE), 1) // 64, BF16)
     lower = ones_where(iota((256, 256), 0) >= iota((256, 256), 1), BF16)
-    auxs = [r_ref[q % 2 * 4 + q // 2, TOK : TOK + AUX, 0:TOK] for q in range(PEERS)]
+    auxs = [r_ref[q % 2 * 4 + q // 2, AT : AT + AUX, 0:TOK] for q in range(PEERS)]
     auxf = [a.astype(F32) for a in auxs]
     starts = [[sum(auxf[2 * y + d][6:7, k : k + 1] for y in range(4)) for k in range(3)] for d in range(2)]
     first = [sum(ones_where(starts[d][k] <= 0.0) for k in range(3)) for d in range(2)]
@@ -153,7 +141,7 @@
         final.append(at + 2048.0 * d)
     for q in range(PEERS):
         code = auxf[q][4:5] * 2048.0 + auxf[q][5:6] + (q // 2) * 256.0
-        bt = jnp.transpose(r_ref[q % 2 * 4 + q // 2, :TOK, WIDE : 2 * WIDE])
+        bt = jnp.transpose(r_ref[q % 2 * 4 + q // 2, TOK:AT, :])
         for d in range(2):
             ends = jnp.broadcast_to(ones_where((code >= final[d]) & (code < 2048.0 * (d + 1))), (16, TOK)).astype(BF16)
             bt_ref[d, :, q * TOK : (q + 1) * TOK] = bt * ends[0:1]
@@ -185,11 +173,11 @@
 
 def inside_kernel(weight_ref, r_ref, got_ref, f_ref, xs_ref, base_ref, cm_ref, b_ref, c_ref):
     weight = rate_lanes(weight_ref)
-    key_rows, key_cols, first, _ = keys_of(r_ref)
+    key_rows, key_cols, first = keys_of(r_ref)
     for q in range(PEERS):
         src = (q % 2) * 4 + q // 2
         sl = slice(q * TOK, (q + 1) * TOK)
-        b_ref[sl, :] = r_ref[src, :TOK, WIDE : 2 * WIDE]
+        b_ref[sl, :] = r_ref[src, TOK:AT, :]
         c = got_ref[src]
         c_ref[sl, :] = c
         for d in range(2):
@@ -286,7 +274,7 @@
     send, send_c = call(
         pack_kernel,
         [HB] * 5,
-        [V((PEERS, TOK + AUX, 2 * WIDE), BF16), pltpu.HBM((PEERS, TOK, WIDE), BF16)],
+        [V((PEERS, AT + AUX, WIDE), BF16), pltpu.HBM((PEERS, TOK, WIDE), BF16)],
         far(tokens[0]), far(pairs), far(step_sizes[0]), far(routes.reshape(1, 16)), far(segments),
         scratch=[
             V((8 * TOK, TOK), BF16),

time: 64.2 us -> 64 us (level)
  no operation moved by 1% of the time
where the time goes in v4:
time: 64 us; the launch traced here: 63.6 us
  blocking collectives  33.8 us (53%)
  starting transfers between devices  13.3 us (21%)
  Pallas kernels  8.25 us (13%)
  waiting for transfers between devices  8.19 us (13%)
    all_to_all x1, blocking collectives, whole(): lax.all_to_all(send, ('dp', 'y'), split_axis=0, concat_axis=0, tiled=True)  21.6 us
    all_to_all x1, blocking collectives, whole(): lax.all_to_all(out, ('dp', 'y'), split_axis=0, concat_axis=0, tiled=True)  12.2 us
    pallas_call x8, Pallas kernels, call(): pl.pallas_call(kernel, in_specs=specs, out_specs=out_specs or [VM] * len(...  8.25 us
    ppermute x1, starting transfers between devices, whole(): e1 = kept(lax.ppermute(e, 'z', [(i, i + 1) for i in range(3)]))  3.53 us
    ppermute x1, starting transfers between devices, whole(): e2 = kept(lax.ppermute(older, 'z', [(i, i + 1) for i in range(1, 3)]))  3.53 us
    all_to_all x1, starting transfers between devices, whole(): lax.all_to_all(send_c, ('dp', 'y'), split_axis=0, concat_axis=0, tiled=True)  3.51 us
    all_to_all x1, waiting for transfers between devices, whole(): lax.all_to_all(send_c, ('dp', 'y'), split_axis=0, concat_axis=0, tiled=True)  3.07 us
    ppermute x1, starting transfers between devices, whole(): others = [kept(lax.ppermute(s0, 'tensor', [(i, i ^ 2) for i in range(4)]))]  2.73 us
  transfers between devices with their start and end apart: 5, of which 4 were waited for; matrix products, arithmetic and copies ran while one was open for 0% of the time, Pallas kernels for 3%

profile of v4, /device:TPU:64, one launch (start us, length us, event | category | flops | bytes accessed | tf_op | source)
XLA Modules:
  0.0 63.6 jit_solution(3344772345244679694)
XLA Ops:
  0.0 2.0 %shard_map.82 = (bf16[8,264,256]{2,1,0:T(8,128)(2,1)S(1)}, bf16[8,128,256]{2,1,0:T(8,128)(2,1)}) custom-call(bf16[128,2048]{1,0:T(8,128)(2,1)} %bitcast.11, bf16[1024,128]{1,0:T(8,128)(2,1)} %bitcast.12, bf16[16,256]{1,0:T(8,128)(2,1)} %bitcast.13, s32[1,16]{1,0:T(1,128)} %bitcast.14, s32[1,256]{1,0:T(1,128)} %seg_ref.1), custom_call_target="tpu_custom_call" | custom-call | tf_op jit(solution)/shard_map/pallas_call | solution.py:261
  2.0 0.0 copy-start.1
  2.0 21.6 %all_to_all.15.r_ref = bf16[8,264,256]{2,1,0:T(8,128)(2,1)S(1)} all-to-all(bf16[8,264,256]{2,1,0:T(8,128)(2,1)S(1)} %get-tuple-element.15), channel_id=1, replica_groups=mesh['dp'=2,'z'=4,'y'=4,'tensor'=4] {'dp','y'}, dimensions={0} | all-to-all | bytes 2162688 | tf_op jit(solution)/shard_map/all_to_all | solution.py:290
  23.6 0.0 copy-done.1
  23.6 0.0 copy-start.2
  23.6 2.4 %shard_map.83 = (bf16[2,264,256]{2,1,0:T(8,128)(2,1)S(1)}, bf16[1024,256]{1,0:T(8,128)(2,1)S(1)}, bf16[1024,256]{1,0:T(8,128)(2,1)S(1)}, f32[2,8,256]{2,1,0:T(8,128)S(1)}) custom-call(f32[32]{0:T(128)S(1)} %copy-done.1, bf16[8,264,256]{2,1,0:T(8,128)(2,1)S(1)} %all_to_all.15.r_ref), custom_call_target="tpu_custom_call" | custom-call | tf_op jit(solution)/shard_map/pallas_call | solution.py:261
  26.0 3.5 %collective-permute-start = (bf16[2,264,256]{2,1,0:T(8,128)(2,1)S(1)}, bf16[2,264,256]{2,1,0:T(8,128)(2,1)S(1)}, u32[]{:S(2)}, u32[]{:S(2)}) collective-permute-start(bf16[2,264,256]{2,1,0:T(8,128)(2,1)S(1)} %get-tuple-element.23), channel_id=1, source_target_pairs={{0,16},{16,32},{32,48},{1,17},{17,33},{33,49},{2,18},{18,34},{34,5... | collective-permute-start | bytes 811016 | tf_op jit(solution)/shard_map/ppermute | solution.py:300
  29.5 3.5 %all-to-all-start.1 = ((bf16[8,128,256]{2,1,0:T(8,128)(2,1)}), bf16[8,128,256]{2,1,0:T(8,128)(2,1)S(1)}, u32[]{:S(2)}, u32[]{:S(2)}) async-start(bf16[8,128,256]{2,1,0:T(8,128)(2,1)} %get-tuple-element.18), calls=%async_computation.1 | async-start | bytes 1048576 | tf_op jit(solution)/shard_map/all_to_all | solution.py:301
  33.0 1.5 %collective-permute-done.e_ref.e1_ref = bf16[2,264,256]{2,1,0:T(8,128)(2,1)S(1)} collective-permute-done((bf16[2,264,256]{2,1,0:T(8,128)(2,1)S(1)}, bf16[2,264,256]{2,1,0:T(8,128)(2,1)S(1)}, u32[]{:S(2)}, u32[]{:S(2)}) %collective-permute-start) | collective-permute-done | bytes 270368 | tf_op jit(solution)/shard_map/ppermute | solution.py:300
  34.6 3.5 %collective-permute-start.1 = (bf16[2,256,256]{2,1,0:T(8,128)(2,1)S(1)}, bf16[2,256,256]{2,1,0:T(8,128)(2,1)S(1)}, u32[]{:S(2)}, u32[]{:S(2)}) collective-permute-start(bf16[2,256,256]{2,1,0:T(8,128)(2,1)S(1)} %shard_map.85), channel_id=1, source_target_pairs={{16,32},{32,48},{17,33},{33,49},{18,34},{34,50},{19,35},{35,51},{2... | collective-permute-start | bytes 786440 | tf_op jit(solution)/shard_map/ppermute | solution.py:303
  38.2 3.1 %all-to-all-done.1.got_ref = bf16[8,128,256]{2,1,0:T(8,128)(2,1)S(1)} async-done(((bf16[8,128,256]{2,1,0:T(8,128)(2,1)}), bf16[8,128,256]{2,1,0:T(8,128)(2,1)S(1)}, u32[]{:S(2)}, u32[]{:S(2)}) %all-to-all-start.1) | async-done | bytes 524320 | tf_op jit(solution)/shard_map/all_to_all | solution.py:301
  41.2 0.0 copy-done.2
  41.2 2.0 %shard_map.84 = (f32[1024,256]{1,0:T(8,128)S(1)}, bf16[1024,512]{1,0:T(8,128)(2,1)S(1)}) custom-call(f32[32]{0:T(128)S(1)} %copy-done.2, bf16[8,264,256]{2,1,0:T(8,128)(2,1)S(1)} %all_to_all.15.r_ref, bf16[8,128,256]{2,1,0:T(8,128)(2,1)S(1)} %all-to-all-done.1.got_ref, bf16[1024,256]{1,0:T(8,128)(2,1)S(1)} %get-tuple-element.19.f_ref, ...), custom_call_target="tpu_custom_call" | custom-call | tf_op jit(solution)/shard_map/pallas_call | solution.py:261
  43.2 0.0 collective-permute-done.1.e2_ref
  43.2 0.5 shard_map.86
  43.7 0.0 copy-start
  43.7 12.2 %all_to_all.16.y_ref.refs_0_ = bf16[8,128,256]{2,1,0:T(8,128)(2,1)S(1)} all-to-all(bf16[8,128,256]{2,1,0:T(8,128)(2,1)S(1)} %shard_map.86), channel_id=1, replica_groups=mesh['dp'=2,'z'=4,'y'=4,'tensor'=4] {'dp','y'}, dimensions={0} | all-to-all | bytes 1048576 | tf_op jit(solution)/shard_map/all_to_all | solution.py:318
  55.9 0.3 shard_map.87.a_ref
  56.1 0.0 collective-permute-start.2
  56.1 1.2 %collective-permute-done.2.b_ref = f32[8,128]{1,0:T(8,128)S(1)} collective-permute-done((f32[8,128]{1,0:T(8,128)S(1)}, f32[8,128]{1,0:T(8,128)S(1)}, u32[]{:S(2)}, u32[]{:S(2)}) %collective-permute-start.2) | collective-permute-done | bytes 4128 | tf_op jit(solution)/shard_map/ppermute | solution.py:320
  57.3 2.7 %collective-permute-start.3 = (f32[8,128]{1,0:T(8,128)S(1)}, f32[8,128]{1,0:T(8,128)S(1)}, u32[]{:S(2)}, u32[]{:S(2)}) collective-permute-start(f32[8,128]{1,0:T(8,128)S(1)} %shard_map.88.refs_1_), channel_id=1, source_target_pairs={{0,2},{1,3},{2,0},{3,1},{4,6},{5,7},{6,4},{7,5},{8,10},{9,11},{10,... | collective-permute-start | bytes 12296 | tf_op jit(solution)/shard_map/ppermute | solution.py:322
  60.1 2.4 %collective-permute-done.3.refs_2_ = f32[8,128]{1,0:T(8,128)S(1)} collective-permute-done((f32[8,128]{1,0:T(8,128)S(1)}, f32[8,128]{1,0:T(8,128)S(1)}, u32[]{:S(2)}, u32[]{:S(2)}) %collective-permute-start.3) | collective-permute-done | bytes 4128 | tf_op jit(solution)/shard_map/ppermute | solution.py:322
  62.4 0.0 copy-done
  62.4 1.2 %shard_map.89 = bf16[128,2048]{1,0:T(8,128)(2,1)} custom-call(bf16[8,128,256]{2,1,0:T(8,128)(2,1)S(1)} %all_to_all.16.y_ref.refs_0_, f32[8,128]{1,0:T(8,128)S(1)} %shard_map.88.refs_1_, f32[8,128]{1,0:T(8,128)S(1)} %collective-permute-done.3.refs_2_, f32[1,2048]{1,0:T(1,128)S(1)} %bitcast.10), custom_call_target="tpu_custom_call" | custom-call | tf_op jit(solution)/shard_map/pallas_call | solution.py:261
  (2 shorter events, 0.1 us)
Async XLA Ops:
  2.0 21.6 %copy-start.1 = (f32[32]{0:T(128)S(1)}, f32[32]{0:T(128)}, u32[]{:S(2)}) copy-start(f32[32]{0:T(128)} %rate_ref.1) | copy-start | bytes 388
  23.6 17.6 %copy-start.2 = (f32[32]{0:T(128)S(1)}, f32[32]{0:T(128)}, u32[]{:S(2)}) copy-start(f32[32]{0:T(128)} %weight_ref.1) | copy-start | bytes 388
  26.0 8.6 %collective-permute-start = (bf16[2,264,256]{2,1,0:T(8,128)(2,1)S(1)}, bf16[2,264,256]{2,1,0:T(8,128)(2,1)S(1)}, u32[]{:S(2)}, u32[]{:S(2)}) collective-permute-start(bf16[2,264,256]{2,1,0:T(8,128)(2,1)S(1)} %get-tuple-element.23), channel_id=1, source_target_pairs={{0,16},{16,32},{32,48},{1,17},{17,33},{33,49},{2,18},{18,34},{34,5... | collective-permute-start | bytes 811016 | tf_op jit(solution)/shard_map/ppermute | solution.py:300
  29.5 11.7 %all-to-all-start.1 = ((bf16[8,128,256]{2,1,0:T(8,128)(2,1)}), bf16[8,128,256]{2,1,0:T(8,128)(2,1)S(1)}, u32[]{:S(2)}, u32[]{:S(2)}) async-start(bf16[8,128,256]{2,1,0:T(8,128)(2,1)} %get-tuple-element.18), calls=%async_computation.1 | async-start | bytes 1048576 | tf_op jit(solution)/shard_map/all_to_all | solution.py:301
  34.6 8.6 %collective-permute-start.1 = (bf16[2,256,256]{2,1,0:T(8,128)(2,1)S(1)}, bf16[2,256,256]{2,1,0:T(8,128)(2,1)S(1)}, u32[]{:S(2)}, u32[]{:S(2)}) collective-permute-start(bf16[2,256,256]{2,1,0:T(8,128)(2,1)S(1)} %shard_map.85), channel_id=1, source_target_pairs={{16,32},{32,48},{17,33},{33,49},{18,34},{34,50},{19,35},{35,51},{2... | collective-permute-start | bytes 786440 | tf_op jit(solution)/shard_map/ppermute | solution.py:303
  43.7 18.8 %copy-start = (f32[2048]{0:T(1024)S(1)}, f32[2048]{0:T(1024)}, u32[]{:S(2)}) copy-start(f32[2048]{0:T(1024)} %param.13) | copy-start | bytes 24580
  56.1 1.2 %collective-permute-start.2 = (f32[8,128]{1,0:T(8,128)S(1)}, f32[8,128]{1,0:T(8,128)S(1)}, u32[]{:S(2)}, u32[]{:S(2)}) collective-permute-start(f32[8,128]{1,0:T(8,128)S(1)} %shard_map.87.a_ref), channel_id=1, source_target_pairs={{0,1},{1,0},{2,3},{3,2},{4,5},{5,4},{6,7},{7,6},{8,9},{9,8},{10,11... | collective-permute-start | bytes 12296 | tf_op jit(solution)/shard_map/ppermute | solution.py:320
  57.3 5.1 %collective-permute-start.3 = (f32[8,128]{1,0:T(8,128)S(1)}, f32[8,128]{1,0:T(8,128)S(1)}, u32[]{:S(2)}, u32[]{:S(2)}) collective-permute-start(f32[8,128]{1,0:T(8,128)S(1)} %shard_map.88.refs_1_), channel_id=1, source_target_pairs={{0,2},{1,3},{2,0},{3,1},{4,6},{5,7},{6,4},{7,5},{8,10},{9,11},{10,... | collective-permute-start | bytes 12296 | tf_op jit(solution)/shard_map/ppermute | solution.py:322

commit v5 on v4

--- a/solution.py
+++ b/solution.py
@@ -113,7 +113,7 @@
     return jnp.where(lane < 32, top, jnp.where(lane < 64, mid, jnp.where(lane < 96, rest - mid, 0.0))).astype(BF16)
 
 
-def state_kernel(rate_ref, r_ref, e_ref, f_ref, xs_ref, own_ref, bt_ref):
+def state_kernel(rate_ref, r_ref, e_ref, v_ref, xs_ref, own_ref, bt_ref, v_buf, sems):
     rate = rate_lanes(rate_ref)
     lane = iota((1, TOK), 1)
     key = lane % 32 // 4
@@ -146,6 +146,7 @@
             ends = jnp.broadcast_to(ones_where((code >= final[d]) & (code < 2048.0 * (d + 1))), (16, TOK)).astype(BF16)
             bt_ref[d, :, q * TOK : (q + 1) * TOK] = bt * ends[0:1]
     total = jnp.zeros((1, TOK), F32)
+    copies = []
     for b in range(4):
         parts = [dot(auxs[2 * b + s], columns, ((0,), (0,))) for s in range(2)]
         part = jnp.concatenate(parts, axis=0)
@@ -154,8 +155,12 @@
         z = jnp.where(mine, part[:, TOK : 2 * TOK], 0.0).astype(BF16)
         sums = dot(lower, z, ((1,), (0,))) + total
         total = sums[255:256]
-        d_wide = dot(three(jnp.where(mine, sums, 0.0), lane), expand, ((1,), (0,)))
-        f_ref[b * 256 : (b + 1) * 256, :] = jnp.exp(-rate * d_wide).astype(BF16)
+        v = three(jnp.where(mine, sums, 0.0), lane)
+        block = slice(b * 256, (b + 1) * 256)
+        v_buf[block, :] = v
+        copies.append(pltpu.make_async_copy(v_buf.at[block, :], v_ref.at[block, :], sems.at[b]))
+        copies[-1].start()
+        d_wide = dot(v, expand, ((1,), (0,)))
         grow = jnp.exp(rate * d_wide) * part[:, 2 * TOK :]
         for s in range(2):
             x = r_ref[s * 4 + b, :TOK, 0:WIDE].astype(F32)
@@ -169,6 +174,16 @@
         e_ref[d, 0:WIDE, :] = e.astype(BF16)
         e_ref[d, WIDE : WIDE + AUX, :] = jnp.broadcast_to(last[d], (AUX, WIDE)).astype(BF16)
         own_ref[d] = jnp.where(row8 == 0, jnp.where(first[d] == last[d], through, 0.0), first[d])
+    for copy in copies:
+        copy.wait()
+
+
+def decay_kernel(rate_ref, v_ref, f_ref):
+    rate = rate_lanes(rate_ref)
+    expand = ones_where(iota((TOK, WIDE), 0) % 4 == iota((TOK, WIDE), 1) // 64, BF16)
+    for b in range(4):
+        sl = slice(b * 256, (b + 1) * 256)
+        f_ref[sl, :] = jnp.exp(-rate * dot(v_ref[sl, :], expand, ((1,), (0,)))).astype(BF16)
 
 
 def inside_kernel(weight_ref, r_ref, got_ref, f_ref, xs_ref, base_ref, cm_ref, b_ref, c_ref):
@@ -288,19 +303,22 @@
         out_specs=[VM, HB],
     )
     got = kept(lax.all_to_all(send, ("dp", "y"), split_axis=0, concat_axis=0, tiled=True))
-    e, f, xs, own = call(
+    e, v, xs, own = call(
         state_kernel,
         [SM, VM],
-        [V((2, WIDE + AUX, WIDE), BF16), V((SPAN, WIDE), BF16), V((SPAN, WIDE), BF16), V((2, AUX, WIDE), F32)],
+        [V((2, WIDE + AUX, WIDE), BF16), pltpu.HBM((SPAN, TOK), BF16), V((SPAN, WIDE), BF16), V((2, AUX, WIDE), F32)],
         decay_rates, got,
-        scratch=[V((2, WIDE, SPAN), BF16)],
-    )
-    f, xs, own = kept(f), kept(xs), kept(own)
+        scratch=[V((2, WIDE, SPAN), BF16), V((SPAN, TOK), BF16), pltpu.SemaphoreType.DMA((4,))],
+        out_specs=[VM, HB, VM, VM],
+    )
+    v, xs, own = far(v), kept(xs), kept(own)
     e, send_c = lax.optimization_barrier((e, send_c))
     e1 = kept(lax.ppermute(e, "z", [(i, i + 1) for i in range(3)]))
     got_c = kept(lax.all_to_all(send_c, ("dp", "y"), split_axis=0, concat_axis=0, tiled=True))
     (older,) = call(pass_kernel, [VM, VM], [V((2, WIDE, WIDE), BF16)], e1, own)
     e2 = kept(lax.ppermute(older, "z", [(i, i + 1) for i in range(1, 3)]))
+    (f,) = call(decay_kernel, [SM, VM], [V((SPAN, WIDE), BF16)], decay_rates, v)
+    f = kept(f)
     base, cm = call(
         inside_kernel,
         [SM] + [VM] * 4,

time: 64 us -> 64.3 us (level)
  Pallas kernels: 8.25 us -> 9.78 us
  waiting for transfers between devices: 8.19 us -> 6.94 us
    pallas_call x8 -> x9, Pallas kernels: 8.25 us -> 9.78 us  [call(): pl.pallas_call(kernel, in_specs=specs, out_specs=out_specs or [VM] * len(...]
    all_to_all x1, waiting for transfers between devices: 3.07 us -> 1.81 us  [whole(): lax.all_to_all(send_c, ('dp', 'y'), split_axis=0, concat_axis=0, tiled=True)]
  transfers between devices with their start and end apart: 5 -> 5, of which waited for: 4 -> 4; matrix products, arithmetic and copies ran while one was open for 0% -> 0% of each run, Pallas kernels for 3% -> 5%
where the time goes in v5:
time: 64.3 us; the launch traced here: 63.9 us
  blocking collectives  33.8 us (53%)
  starting transfers between devices  13.3 us (21%)
  Pallas kernels  9.78 us (15%)
  waiting for transfers between devices  6.94 us (11%)
    all_to_all x1, blocking collectives, whole(): lax.all_to_all(send, ('dp', 'y'), split_axis=0, concat_axis=0, tiled=True)  21.6 us
    all_to_all x1, blocking collectives, whole(): lax.all_to_all(out, ('dp', 'y'), split_axis=0, concat_axis=0, tiled=True)  12.2 us
    pallas_call x9, Pallas kernels, call(): pl.pallas_call(kernel, in_specs=specs, out_specs=out_specs or [VM] * len(...  9.78 us
    ppermute x1, starting transfers between devices, whole(): e1 = kept(lax.ppermute(e, 'z', [(i, i + 1) for i in range(3)]))  3.53 us
    ppermute x1, starting transfers between devices, whole(): e2 = kept(lax.ppermute(older, 'z', [(i, i + 1) for i in range(1, 3)]))  3.53 us
    all_to_all x1, starting transfers between devices, whole(): lax.all_to_all(send_c, ('dp', 'y'), split_axis=0, concat_axis=0, tiled=True)  3.51 us
    ppermute x1, starting transfers between devices, whole(): others = [kept(lax.ppermute(s0, 'tensor', [(i, i ^ 2) for i in range(4)]))]  2.73 us
    ppermute x1, waiting for transfers between devices, whole(): others = [kept(lax.ppermute(s0, 'tensor', [(i, i ^ 2) for i in range(4)]))]  2.38 us
  transfers between devices with their start and end apart: 5, of which 4 were waited for; matrix products, arithmetic and copies ran while one was open for 0% of the time, Pallas kernels for 5%

profile of v5, /device:TPU:64, one launch (start us, length us, event | category | flops | bytes accessed | tf_op | source)
XLA Modules:
  0.0 63.9 jit_solution(16447919505059555855)
XLA Ops:
  0.0 2.0 %shard_map.82 = (bf16[8,264,256]{2,1,0:T(8,128)(2,1)S(1)}, bf16[8,128,256]{2,1,0:T(8,128)(2,1)}) custom-call(bf16[128,2048]{1,0:T(8,128)(2,1)} %bitcast.11, bf16[1024,128]{1,0:T(8,128)(2,1)} %bitcast.12, bf16[16,256]{1,0:T(8,128)(2,1)} %bitcast.13, s32[1,16]{1,0:T(1,128)} %bitcast.14, s32[1,256]{1,0:T(1,128)} %seg_ref.1), custom_call_target="tpu_custom_call" | custom-call | tf_op jit(solution)/shard_map/pallas_call | solution.py:276
  2.0 0.0 copy-start.1
  2.0 21.6 %all_to_all.15.r_ref = bf16[8,264,256]{2,1,0:T(8,128)(2,1)S(1)} all-to-all(bf16[8,264,256]{2,1,0:T(8,128)(2,1)S(1)} %get-tuple-element.15), channel_id=1, replica_groups=mesh['dp'=2,'z'=4,'y'=4,'tensor'=4] {'dp','y'}, dimensions={0} | all-to-all | bytes 2162688 | tf_op jit(solution)/shard_map/all_to_all | solution.py:305
  23.6 0.0 copy-done.1
  23.6 2.6 %shard_map.83 = (bf16[2,264,256]{2,1,0:T(8,128)(2,1)S(1)}, bf16[1024,128]{1,0:T(8,128)(2,1)}, bf16[1024,256]{1,0:T(8,128)(2,1)S(1)}, f32[2,8,256]{2,1,0:T(8,128)S(1)}) custom-call(f32[32]{0:T(128)S(1)} %copy-done.1, bf16[8,264,256]{2,1,0:T(8,128)(2,1)S(1)} %all_to_all.15.r_ref), custom_call_target="tpu_custom_call" | custom-call | tf_op jit(solution)/shard_map/pallas_call | solution.py:276
  26.2 0.0 copy-start.2
  26.3 3.5 %collective-permute-start = (bf16[2,264,256]{2,1,0:T(8,128)(2,1)S(1)}, bf16[2,264,256]{2,1,0:T(8,128)(2,1)S(1)}, u32[]{:S(2)}, u32[]{:S(2)}) collective-permute-start(bf16[2,264,256]{2,1,0:T(8,128)(2,1)S(1)} %get-tuple-element.23), channel_id=1, source_target_pairs={{0,16},{16,32},{32,48},{1,17},{17,33},{33,49},{2,18},{18,34},{34,5... | collective-permute-start | bytes 811016 | tf_op jit(solution)/shard_map/ppermute | solution.py:316
  29.8 3.5 %all-to-all-start.1 = ((bf16[8,128,256]{2,1,0:T(8,128)(2,1)}), bf16[8,128,256]{2,1,0:T(8,128)(2,1)S(1)}, u32[]{:S(2)}, u32[]{:S(2)}) async-start(bf16[8,128,256]{2,1,0:T(8,128)(2,1)} %get-tuple-element.18), calls=%async_computation.1 | async-start | bytes 1048576 | tf_op jit(solution)/shard_map/all_to_all | solution.py:317
  33.3 1.5 %collective-permute-done.e_ref.e1_ref = bf16[2,264,256]{2,1,0:T(8,128)(2,1)S(1)} collective-permute-done((bf16[2,264,256]{2,1,0:T(8,128)(2,1)S(1)}, bf16[2,264,256]{2,1,0:T(8,128)(2,1)S(1)}, u32[]{:S(2)}, u32[]{:S(2)}) %collective-permute-start) | collective-permute-done | bytes 270368 | tf_op jit(solution)/shard_map/ppermute | solution.py:316
  34.9 3.5 %collective-permute-start.1 = (bf16[2,256,256]{2,1,0:T(8,128)(2,1)S(1)}, bf16[2,256,256]{2,1,0:T(8,128)(2,1)S(1)}, u32[]{:S(2)}, u32[]{:S(2)}) collective-permute-start(bf16[2,256,256]{2,1,0:T(8,128)(2,1)S(1)} %shard_map.86), channel_id=1, source_target_pairs={{16,32},{32,48},{17,33},{33,49},{18,34},{34,50},{19,35},{35,51},{2... | collective-permute-start | bytes 786440 | tf_op jit(solution)/shard_map/ppermute | solution.py:319
  38.5 1.3 %shard_map.84.f_ref = bf16[1024,256]{1,0:T(8,128)(2,1)S(1)} custom-call(f32[32]{0:T(128)S(1)} %copy-done.1, bf16[1024,128]{1,0:T(8,128)(2,1)} %get-tuple-element.19.v_ref), custom_call_target="tpu_custom_call" | custom-call | tf_op jit(solution)/shard_map/pallas_call | solution.py:276
  39.7 1.8 %all-to-all-done.1.got_ref = bf16[8,128,256]{2,1,0:T(8,128)(2,1)S(1)} async-done(((bf16[8,128,256]{2,1,0:T(8,128)(2,1)}), bf16[8,128,256]{2,1,0:T(8,128)(2,1)S(1)}, u32[]{:S(2)}, u32[]{:S(2)}) %all-to-all-start.1) | async-done | bytes 524320 | tf_op jit(solution)/shard_map/all_to_all | solution.py:317
  41.5 0.0 copy-done.2
  41.5 1.9 %shard_map.85 = (f32[1024,256]{1,0:T(8,128)S(1)}, bf16[1024,512]{1,0:T(8,128)(2,1)S(1)}) custom-call(f32[32]{0:T(128)S(1)} %copy-done.2, bf16[8,264,256]{2,1,0:T(8,128)(2,1)S(1)} %all_to_all.15.r_ref, bf16[8,128,256]{2,1,0:T(8,128)(2,1)S(1)} %all-to-all-done.1.got_ref, bf16[1024,256]{1,0:T(8,128)(2,1)S(1)} %shard_map.84.f_ref, ...), custom_call_target="tpu_custom_call" | custom-call | tf_op jit(solution)/shard_map/pallas_call | solution.py:276
  43.5 0.0 collective-permute-done.1.e2_ref
  43.5 0.5 shard_map.87
  44.0 0.0 copy-start
  44.0 12.2 %all_to_all.16.y_ref.refs_0_ = bf16[8,128,256]{2,1,0:T(8,128)(2,1)S(1)} all-to-all(bf16[8,128,256]{2,1,0:T(8,128)(2,1)S(1)} %shard_map.87), channel_id=1, replica_groups=mesh['dp'=2,'z'=4,'y'=4,'tensor'=4] {'dp','y'}, dimensions={0} | all-to-all | bytes 1048576 | tf_op jit(solution)/shard_map/all_to_all | solution.py:336
  56.2 0.3 shard_map.88.a_ref
  56.4 0.0 collective-permute-start.2
  56.4 1.2 %collective-permute-done.2.b_ref = f32[8,128]{1,0:T(8,128)S(1)} collective-permute-done((f32[8,128]{1,0:T(8,128)S(1)}, f32[8,128]{1,0:T(8,128)S(1)}, u32[]{:S(2)}, u32[]{:S(2)}) %collective-permute-start.2) | collective-permute-done | bytes 4128 | tf_op jit(solution)/shard_map/ppermute | solution.py:338
  57.6 2.7 %collective-permute-start.3 = (f32[8,128]{1,0:T(8,128)S(1)}, f32[8,128]{1,0:T(8,128)S(1)}, u32[]{:S(2)}, u32[]{:S(2)}) collective-permute-start(f32[8,128]{1,0:T(8,128)S(1)} %shard_map.89.refs_1_), channel_id=1, source_target_pairs={{0,2},{1,3},{2,0},{3,1},{4,6},{5,7},{6,4},{7,5},{8,10},{9,11},{10,... | collective-permute-start | bytes 12296 | tf_op jit(solution)/shard_map/ppermute | solution.py:340
  60.4 2.4 %collective-permute-done.3.refs_2_ = f32[8,128]{1,0:T(8,128)S(1)} collective-permute-done((f32[8,128]{1,0:T(8,128)S(1)}, f32[8,128]{1,0:T(8,128)S(1)}, u32[]{:S(2)}, u32[]{:S(2)}) %collective-permute-start.3) | collective-permute-done | bytes 4128 | tf_op jit(solution)/shard_map/ppermute | solution.py:340
  62.8 0.0 copy-done
  62.8 1.2 %shard_map.90 = bf16[128,2048]{1,0:T(8,128)(2,1)} custom-call(bf16[8,128,256]{2,1,0:T(8,128)(2,1)S(1)} %all_to_all.16.y_ref.refs_0_, f32[8,128]{1,0:T(8,128)S(1)} %shard_map.89.refs_1_, f32[8,128]{1,0:T(8,128)S(1)} %collective-permute-done.3.refs_2_, f32[1,2048]{1,0:T(1,128)S(1)} %bitcast.10), custom_call_target="tpu_custom_call" | custom-call | tf_op jit(solution)/shard_map/pallas_call | solution.py:276
  (2 shorter events, 0.1 us)
Async XLA Ops:
  2.0 21.6 %copy-start.1 = (f32[32]{0:T(128)S(1)}, f32[32]{0:T(128)}, u32[]{:S(2)}) copy-start(f32[32]{0:T(128)} %rate_ref.3) | copy-start | bytes 388
  26.2 15.3 %copy-start.2 = (f32[32]{0:T(128)S(1)}, f32[32]{0:T(128)}, u32[]{:S(2)}) copy-start(f32[32]{0:T(128)} %weight_ref.1) | copy-start | bytes 388
  26.3 8.6 %collective-permute-start = (bf16[2,264,256]{2,1,0:T(8,128)(2,1)S(1)}, bf16[2,264,256]{2,1,0:T(8,128)(2,1)S(1)}, u32[]{:S(2)}, u32[]{:S(2)}) collective-permute-start(bf16[2,264,256]{2,1,0:T(8,128)(2,1)S(1)} %get-tuple-element.23), channel_id=1, source_target_pairs={{0,16},{16,32},{32,48},{1,17},{17,33},{33,49},{2,18},{18,34},{34,5... | collective-permute-start | bytes 811016 | tf_op jit(solution)/shard_map/ppermute | solution.py:316
  29.8 11.7 %all-to-all-start.1 = ((bf16[8,128,256]{2,1,0:T(8,128)(2,1)}), bf16[8,128,256]{2,1,0:T(8,128)(2,1)S(1)}, u32[]{:S(2)}, u32[]{:S(2)}) async-start(bf16[8,128,256]{2,1,0:T(8,128)(2,1)} %get-tuple-element.18), calls=%async_computation.1 | async-start | bytes 1048576 | tf_op jit(solution)/shard_map/all_to_all | solution.py:317
  34.9 8.6 %collective-permute-start.1 = (bf16[2,256,256]{2,1,0:T(8,128)(2,1)S(1)}, bf16[2,256,256]{2,1,0:T(8,128)(2,1)S(1)}, u32[]{:S(2)}, u32[]{:S(2)}) collective-permute-start(bf16[2,256,256]{2,1,0:T(8,128)(2,1)S(1)} %shard_map.86), channel_id=1, source_target_pairs={{16,32},{32,48},{17,33},{33,49},{18,34},{34,50},{19,35},{35,51},{2... | collective-permute-start | bytes 786440 | tf_op jit(solution)/shard_map/ppermute | solution.py:319
  44.0 18.8 %copy-start = (f32[2048]{0:T(1024)S(1)}, f32[2048]{0:T(1024)}, u32[]{:S(2)}) copy-start(f32[2048]{0:T(1024)} %param.13) | copy-start | bytes 24580
  56.4 1.2 %collective-permute-start.2 = (f32[8,128]{1,0:T(8,128)S(1)}, f32[8,128]{1,0:T(8,128)S(1)}, u32[]{:S(2)}, u32[]{:S(2)}) collective-permute-start(f32[8,128]{1,0:T(8,128)S(1)} %shard_map.88.a_ref), channel_id=1, source_target_pairs={{0,1},{1,0},{2,3},{3,2},{4,5},{5,4},{6,7},{7,6},{8,9},{9,8},{10,11... | collective-permute-start | bytes 12296 | tf_op jit(solution)/shard_map/ppermute | solution.py:338
  57.6 5.1 %collective-permute-start.3 = (f32[8,128]{1,0:T(8,128)S(1)}, f32[8,128]{1,0:T(8,128)S(1)}, u32[]{:S(2)}, u32[]{:S(2)}) collective-permute-start(f32[8,128]{1,0:T(8,128)S(1)} %shard_map.89.refs_1_), channel_id=1, source_target_pairs={{0,2},{1,3},{2,0},{3,1},{4,6},{5,7},{6,4},{7,5},{8,10},{9,11},{10,... | collective-permute-start | bytes 12296 | tf_op jit(solution)/shard_map/ppermute | solution.py:340
